TPU v7x, 512 devices: a whole 4x4x16 slice. The times are simulated.
512 devices in a mesh: gx: 32 (over z, core), gy: 16 (over y, x).
Axes of the slice: x: 4, y: 4, z: 16, core: 2. Of those that a mesh axis runs over, the one named last changes fastest.
Arguments:
- tokens: bfloat16 [8192, 2048], P('gx'), may hold values from -6 to 6
- lengths: int32 [4], replicated, may hold values from 1 to 4096, 8192 in all
- adapter_of_request: int32 [4], replicated, may hold values from 0 to 15
- adapter_storage_slot: int32 [16], replicated, may hold values from 0 to 15, each once
- page_cache_slot: int32 [1024], P('gx'), may hold values from 0 to 1023, as said below
- query_key_value_weight: bfloat16 [2048, 16, 384], P(None, 'gy'), may hold values from -4 to 4
- adapter_down_maps: bfloat16 [16, 2048, 48], P('gy'), may hold values from -0.125 to 0.125
- adapter_up_maps: bfloat16 [16, 3, 16, 16, 128], P(None, None, None, 'gy'), may hold values from -1.5 to 1.5
- query_norm_gain: float32 [16, 128], P('gy'), may hold values from 0.25 to 1.75
- key_norm_gain: float32 [16, 128], P('gy'), may hold values from 0.25 to 1.75
- output_weight: bfloat16 [16, 128, 2048], P('gy'), may hold values from -0.125 to 0.125
- post_norm_gain: float32 [2048], replicated, may hold values from 0.25 to 1.75
Outputs:
- mixed: bfloat16 [8192, 2048], P('gx')
- kv_cache: bfloat16 [1024, 8, 16, 256], P('gx', None, 'gy')
Inputs may be any that keep to these rules, and one draw needn't show every extreme that they name: `page_cache_slot`: each slot appears once; the 32 pages of the tokens of one index of gx have exactly 1 slot among the 32 slots held by each index k of gx (slots k * 32 onward).
All inputs are finite; a program needn't handle non-finite values.
Results may differ from a plain program's by a relative error of at most 0.017.
Values may be sent and summed in bfloat16 or wider, within the bound.
No kernel may reach another device: no remote copies, remote signals or barrier semaphores. Data moves between devices by JAX's collectives and lax.ppermute only.
A program may use at most 64 MiB of HBM per device.

v0:
```python
import jax
import jax.numpy as jnp
from jax import lax
from jax.sharding import PartitionSpec as P

MODEL_WIDTH = 2048
HEAD_SIZE = 128
ADAPTER_RANK = 16
PAGE = 8


def request_of(rows, ends):
    return jnp.sum((ends[None, :] <= rows[:, None]).astype(jnp.int32), axis=1)


def lookup(index, table):
    match = index[:, None] == jnp.arange(table.shape[0])[None, :]
    return jnp.sum(jnp.where(match, table[None, :], 0), axis=1)


def rotate(values, positions):
    half = values.shape[-1] // 2
    freq = 500000.0 ** (-(jnp.arange(half).astype(jnp.float32) * 2.0) / values.shape[-1])
    angle = positions.astype(jnp.float32)[:, None] * freq[None, :]
    cosine = jnp.cos(angle)[:, None, :]
    sine = jnp.sin(angle)[:, None, :]
    first = values[..., :half]
    second = values[..., half:]
    return jnp.concatenate(
        [first * cosine - second * sine, second * cosine + first * sine], axis=-1
    )


def shards(
    tokens,
    lengths,
    adapter_of_request,
    adapter_storage_slot,
    page_cache_slot,
    query_key_value_weight,
    adapter_down_maps,
    adapter_up_maps,
    query_norm_gain,
    key_norm_gain,
    output_weight,
    post_norm_gain,
):
    count = tokens.shape[0]
    group = lax.axis_index("gx")
    member = lax.axis_index("gy")
    rows = group * count + jnp.arange(count)
    ends = jnp.cumsum(lengths)
    starts = ends - lengths
    request = request_of(rows, ends)
    positions = rows - lookup(request, starts)
    slots = lookup(lookup(request, adapter_of_request), adapter_storage_slot)
    resident_count = adapter_down_maps.shape[0]
    held = member * resident_count + jnp.arange(resident_count)
    reduced_rows = jnp.einsum(
        "zm,ump->zup", tokens, adapter_down_maps, preferred_element_type=jnp.float32
    )
    chosen = (slots[:, None] == held[None, :]).astype(jnp.float32)
    partial_low = jnp.sum(chosen[:, :, None] * reduced_rows, axis=1)
    low = lax.psum(partial_low.astype(jnp.bfloat16), "gy")
    adapter_count_total = adapter_up_maps.shape[0]
    selector = (slots[:, None] == jnp.arange(adapter_count_total)[None, :]).astype(jnp.bfloat16)
    expanded_rows = selector[:, :, None, None] * low.reshape(count, 1, 3, ADAPTER_RANK)
    adapter_update = jnp.einsum(
        "dzqi,zqibj->dqbj", expanded_rows, adapter_up_maps, preferred_element_type=jnp.float32
    )
    base = jnp.einsum(
        "td,dhe->the", tokens, query_key_value_weight, preferred_element_type=jnp.float32
    )
    query = base[..., :HEAD_SIZE] + adapter_update[:, 0]
    key_raw = base[..., HEAD_SIZE : 2 * HEAD_SIZE] + adapter_update[:, 1]
    value = base[..., 2 * HEAD_SIZE :] + adapter_update[:, 2]
    query_sq, key_sq = lax.psum(
        (jnp.sum(query * query, axis=(1, 2)), jnp.sum(key_raw * key_raw, axis=(1, 2))), "gy"
    )
    query_n = (
        query * lax.rsqrt(query_sq / MODEL_WIDTH + 1e-06)[:, None, None] * query_norm_gain[None]
    )
    key_n = key_raw * lax.rsqrt(key_sq / MODEL_WIDTH + 1e-06)[:, None, None] * key_norm_gain[None]
    query_b = rotate(query_n, positions).astype(jnp.bfloat16)
    key_b = rotate(key_n, positions).astype(jnp.bfloat16)
    value_b = value.astype(jnp.bfloat16)
    heads_here = query_key_value_weight.shape[1]
    pages_here = count // PAGE
    pages = jnp.concatenate([key_b, value_b], axis=-1).reshape(
        pages_here, PAGE, heads_here, 2 * HEAD_SIZE
    )
    order = jnp.argsort(page_cache_slot)
    got_pages, got_slots = (
        lax.all_to_all(pages[order], "gx", split_axis=0, concat_axis=0, tiled=True),
        lax.all_to_all(page_cache_slot[order], "gx", split_axis=0, concat_axis=0, tiled=True),
    )
    kv_cache = got_pages[jnp.argsort(got_slots)]
    scale = HEAD_SIZE ** (-0.5)

    def attend(carry, key_vectors, values, key_rows):
        best, total, accum = carry
        key_request = request_of(key_rows, ends)
        scores = (
            jnp.einsum("the,khe->htk", query_b, key_vectors, preferred_element_type=jnp.float32)
            * scale
        )
        allowed = (request[:, None] == key_request[None, :]) & (key_rows[None, :] <= rows[:, None])
        masked = jnp.where(allowed[None], scores, -1e30)
        new_best = jnp.maximum(best, jnp.max(masked, axis=-1))
        weights = jnp.where(allowed[None], jnp.exp(scores - new_best[..., None]), 0.0)
        factor = jnp.exp(best - new_best)
        total = total * factor + jnp.sum(weights, axis=-1)
        update = jnp.einsum(
            "htk,khe->hte", weights.astype(jnp.bfloat16), values, preferred_element_type=jnp.float32
        )
        accum = accum * factor[..., None] + update
        return (new_best, total, accum)

    initial = (
        jnp.full((heads_here, count), -1e30, jnp.float32),
        jnp.zeros((heads_here, count), jnp.float32),
        jnp.zeros((heads_here, count, HEAD_SIZE), jnp.float32),
    )
    key_vectors = lax.all_gather(key_b, "gx", axis=0, tiled=True)
    values = lax.all_gather(value_b, "gx", axis=0, tiled=True)
    size = key_vectors.shape[0]
    block = 512

    def one_block(index, state):
        begin = index * block
        key_part = lax.dynamic_slice_in_dim(key_vectors, begin, block, 0)
        value_part = lax.dynamic_slice_in_dim(values, begin, block, 0)
        key_rows = begin + jnp.arange(block)
        return attend(state, key_part, value_part, key_rows)

    best, total, accum = lax.fori_loop(0, size // block, one_block, initial)
    attn = (accum / total[..., None]).astype(jnp.bfloat16)
    partial_out = jnp.einsum("hte,hed->td", attn, output_weight, preferred_element_type=jnp.float32)
    output = lax.psum(partial_out.astype(jnp.bfloat16), "gy").astype(jnp.float32)
    normed = (
        output
        * lax.rsqrt(jnp.mean(output * output, axis=1) + 1e-06)[:, None]
        * post_norm_gain[None, :]
    )
    mixed = (tokens.astype(jnp.float32) + normed).astype(jnp.bfloat16)
    return (mixed, kv_cache)


def solution(mesh):
    return jax.shard_map(
        shards,
        mesh=mesh,
        in_specs=(
            P("gx", None),
            P(),
            P(),
            P(),
            P("gx"),
            P(None, "gy", None),
            P("gy", None, None),
            P(None, None, None, "gy", None),
            P("gy", None),
            P("gy", None),
            P("gy", None, None),
            P(),
        ),
        out_specs=(P("gx", None), P("gx", None, "gy", None)),
        check_vma=False,
    )
```

profile of v0, /device:TPU:1, one launch (start us, length us, event | category | flops | bytes accessed | tf_op | source)
XLA Modules:
  0.0 444.7 jit_solution(11517718805805738873)
XLA Ops:
  10.4 1.7 fusion.33
  12.2 61.6 %psum.28 = bf16[256,3,16]{0,2,1:T(8,128)(2,1)S(1)} all-reduce(bf16[256,3,16]{0,2,1:T(8,128)(2,1)S(1)} %bitcast.114), channel_id=1, replica_groups=mesh['gx'=32,'gy'=16] {'gy'}, use_global_device_ids=true, to_apply=%region_4.5 | all-reduce | flops 12288 | bytes 49152 | tf_op jit(solution)/shard_map/psum | solution.py:64
  73.8 1.9 fusion.30
  76.2 28.5 %all-reduce = (f32[256]{0:T(256)S(1)}, f32[256]{0:T(256)S(1)}) all-reduce(f32[256]{0:T(256)S(1)} %get-tuple-element.231, f32[256]{0:T(256)S(1)} %get-tuple-element.230), channel_id=1, replica_groups=mesh['gx'=32,'gy'=16] {'gy'}, use_global_device_ids=true, to_apply=%region_6.7 | all-reduce | flops 512 | bytes 4096 | tf_op jit(solution)/shard_map/psum | solution.py:77
  107.8 93.1 %all-gather.3.cloned.1.call-done = bf16[8192,1,128]{2,0,1:T(8,128)(2,1)} async-done(((bf16[256,1,128]{2,0,1:T(8,128)(2,1)}), bf16[8192,1,128]{2,0,1:T(8,128)(2,1)}) %all-gather.3.cloned.1.call-update) | async-done | bytes 2097168 | tf_op jit(solution)/shard_map/all_gather | solution.py:124
  200.8 71.5 %all-gather.5.cloned.1.call-done = bf16[8192,1,128]{2,0,1:T(8,128)(2,1)} async-done(((bf16[256,1,128]{2,0,1:T(8,128)(2,1)}), bf16[8192,1,128]{2,0,1:T(8,128)(2,1)}) %all-gather.5.cloned.1.call-update) | async-done | bytes 2097168 | tf_op jit(solution)/shard_map/all_gather | solution.py:125
  272.3 47.3 %while.18 = (s32[]{:T(128)}, f32[1,256]{1,0:T(1,128)S(1)}, f32[1,256]{1,0:T(1,128)S(1)}, f32[1,256,128]{2,1,0:T(8,128)S(1)}, s32[256]{0:T(256)S(1)}, /*index=5*/...) while((s32[]{:T(128)}, f32[1,256]{1,0:T(1,128)S(1)}, ...), condition=%wide.region_14.15_spmd.clone, body=%wide.region_10.14_spmd.clone.sunk | while | flops 69574144 | bytes 2204895 | solution.py:136
  272.4 1.2 select_reduce_fusion.5
  273.9 1.4 fusion.75
  275.4 1.2 select_reduce_fusion.5
  276.9 1.4 fusion.75
  278.4 1.2 select_reduce_fusion.5
  279.8 1.4 fusion.75
  281.3 1.2 select_reduce_fusion.5
  282.8 1.4 fusion.75
  284.3 1.2 select_reduce_fusion.5
  285.7 1.4 fusion.75
  287.2 1.2 select_reduce_fusion.5
  288.7 1.4 fusion.75
  290.2 1.2 select_reduce_fusion.5
  291.6 1.4 fusion.75
  293.1 1.2 select_reduce_fusion.5
  294.6 1.4 fusion.75
  296.1 1.2 select_reduce_fusion.5
  297.5 1.4 fusion.75
  299.0 1.2 select_reduce_fusion.5
  300.5 1.4 fusion.75
  302.0 1.2 select_reduce_fusion.5
  303.4 1.4 fusion.75
  306.4 1.4 fusion.75
  307.9 1.2 select_reduce_fusion.5
  309.3 1.4 fusion.75
  312.3 1.4 fusion.75
  313.8 1.2 select_reduce_fusion.5
  315.2 1.4 fusion.75
  318.2 1.4 fusion.75
  319.6 1.5 convolution_convert_fusion
  321.1 1.7 sort.31
  324.2 8.2 %all-to-all-start.1 = ((s32[32,1,1]{2,1,0:T(1,128)}), s32[32,1,1]{2,1,0:T(1,128)S(1)}, u32[]{:S(2)}, u32[]{:S(2)}) async-start(s32[32,1,1]{2,1,0:T(1,128)} %copy.31), calls=%async_computation.1 | async-start | bytes 32768 | tf_op jit(solution)/shard_map/all_to_all | solution.py:95
  332.6 1.2 gather_fusion
  333.8 10.4 %all-to-all-done.1 = s32[32,1,1]{2,1,0:T(1,128)S(1)} async-done(((s32[32,1,1]{2,1,0:T(1,128)}), s32[32,1,1]{2,1,0:T(1,128)S(1)}, u32[]{:S(2)}, u32[]{:S(2)}) %all-to-all-start.1) | async-done | bytes 160 | tf_op jit(solution)/shard_map/all_to_all | solution.py:95
  344.2 4.5 %all-to-all-start = ((bf16[32,8,1,256]{3,1,2,0:T(8,128)(2,1)}), bf16[32,8,1,256]{3,1,2,0:T(8,128)(2,1)S(1)}, u32[]{:S(2)}, u32[]{:S(2)}) async-start(bf16[32,8,1,256]{3,1,2,0:T(8,128)(2,1)} %bitcast.26), calls=%async_computation | async-start | bytes 262144 | tf_op jit(solution)/shard_map/all_to_all | solution.py:94
  349.3 1.7 sort.32
  351.0 13.8 %all-to-all-done = bf16[32,8,1,256]{3,1,2,0:T(8,128)(2,1)S(1)} async-done(((bf16[32,8,1,256]{3,1,2,0:T(8,128)(2,1)}), bf16[32,8,1,256]{3,1,2,0:T(8,128)(2,1)S(1)}, u32[]{:S(2)}, u32[]{:S(2)}) %all-to-all-start) | async-done | bytes 131104 | tf_op jit(solution)/shard_map/all_to_all | solution.py:94
  364.8 1.2 gather_fusion.2
  366.1 68.0 %all-reduce.3.cloned.1.call-done = bf16[256,2048]{1,0:T(8,128)(2,1)} async-done(((bf16[256,2048]{1,0:T(8,128)(2,1)}), bf16[256,2048]{1,0:T(8,128)(2,1)}) %all-reduce.3.cloned.1.call-update) | async-done | bytes 1048592 | tf_op jit(solution)/shard_map/psum | solution.py:139
  434.0 1.5 fusion.24
  435.6 2.6 fusion.27
  (170 shorter events, 17.8 us)
Async XLA Ops:
  7.2 66.6 %copy-start = (bf16[2048,1,384]{2,0,1:T(8,128)(2,1)S(1)}, bf16[2048,1,384]{2,0,1:T(8,128)(2,1)}, u32[]{:S(2)}) copy-start(bf16[2048,1,384]{2,0,1:T(8,128)(2,1)} %param.19) | copy-start | bytes 4718596
  7.2 193.6 %all-gather.3.cloned.1.call-start = ((), (), s32[]{:S(2)}) async-start(), calls=%async_computation.2 | async-start | bytes 2162688 | tf_op jit(solution)/shard_map/all_gather | solution.py:124
  10.4 65.3 %copy-start.8 = (bf16[16,3,16,1,128]{4,2,3,1,0:T(8,128)(2,1)S(1)}, bf16[16,3,16,1,128]{4,2,3,1,0:T(8,128)(2,1)}, u32[]{:S(2)}) copy-start(bf16[16,3,16,1,128]{4,2,3,1,0:T(8,128)(2,1)} %param.21) | copy-start | bytes 589828
  75.7 29.0 %copy-start.6 = (f32[1,128]{1,0:T(1,128)S(1)}, f32[1,128]{1,0:T(1,128)}, u32[]{:S(2)}) copy-start(f32[1,128]{1,0:T(1,128)} %param.23) | copy-start | bytes 1540
  75.7 29.0 %copy-start.7 = (f32[1,128]{1,0:T(1,128)S(1)}, f32[1,128]{1,0:T(1,128)}, u32[]{:S(2)}) copy-start(f32[1,128]{1,0:T(1,128)} %param.22) | copy-start | bytes 1540
  106.8 165.5 %all-gather.5.cloned.1.call-start = ((), (), s32[]{:S(2)}) async-start(), calls=%async_computation.3 | async-start | bytes 2162688 | tf_op jit(solution)/shard_map/all_gather | solution.py:125
  107.6 326.4 %all-reduce.3.cloned.1.call-start = ((), (), s32[]{:S(2)}) async-start(), calls=%async_computation.4 | async-start | bytes 2097152 | tf_op jit(solution)/shard_map/psum | solution.py:139
  272.3 47.3 %copy-start.4 = (bf16[1,128,2048]{2,1,0:T(8,128)(2,1)S(1)}, bf16[1,128,2048]{2,1,0:T(8,128)(2,1)}, u32[]{:S(2)}) copy-start(bf16[1,128,2048]{2,1,0:T(8,128)(2,1)} %param.24) | copy-start | bytes 1572868
  319.6 1.5 copy-start.1
  319.6 12.9 %copy-start.3 = (bf16[256,1,128]{2,0,1:T(8,128)(2,1)S(1)}, bf16[256,1,128]{2,0,1:T(8,128)(2,1)}, u32[]{:S(2)}) copy-start(bf16[256,1,128]{2,0,1:T(8,128)(2,1)} %get-tuple-element.260) | copy-start | bytes 196612
  321.1 114.5 %copy-start.2 = (bf16[256,2048]{1,0:T(8,128)(2,1)S(1)}, bf16[256,2048]{1,0:T(8,128)(2,1)}, u32[]{:S(2)}) copy-start(bf16[256,2048]{1,0:T(8,128)(2,1)} %param.14) | copy-start | bytes 3145732
  321.1 114.5 %copy-start.5 = (f32[2048]{0:T(1024)S(1)}, f32[2048]{0:T(1024)}, u32[]{:S(2)}) copy-start(f32[2048]{0:T(1024)} %param.25) | copy-start | bytes 24580
  324.2 20.0 %all-to-all-start.1 = ((s32[32,1,1]{2,1,0:T(1,128)}), s32[32,1,1]{2,1,0:T(1,128)S(1)}, u32[]{:S(2)}, u32[]{:S(2)}) async-start(s32[32,1,1]{2,1,0:T(1,128)} %copy.31), calls=%async_computation.1 | async-start | bytes 32768 | tf_op jit(solution)/shard_map/all_to_all | solution.py:95
  344.2 20.6 %all-to-all-start = ((bf16[32,8,1,256]{3,1,2,0:T(8,128)(2,1)}), bf16[32,8,1,256]{3,1,2,0:T(8,128)(2,1)S(1)}, u32[]{:S(2)}, u32[]{:S(2)}) async-start(bf16[32,8,1,256]{3,1,2,0:T(8,128)(2,1)} %bitcast.26), calls=%async_computation | async-start | bytes 262144 | tf_op jit(solution)/shard_map/all_to_all | solution.py:94
Sparse Core Ops, SparseCore 0:
  107.0 93.8 all-gather.2
  203.5 68.7 all-gather.4
  321.2 112.7 all-reduce.2
where the time goes:
time: 446 us; the launch traced here: 445 us
  waiting for transfers between devices  257 us (58%)
  blocking collectives  90.1 us (20%)
  matrix products  46.3 us (10%)
  other arithmetic  19.1 us (4%)
  between operations  14 us (3%)
  starting transfers between devices  12.8 us (3%)
    all_gather x1, waiting for transfers between devices, shards(): key_vectors = lax.all_gather(key_b, 'gx', axis=0, tiled=True)  93.1 us
    all_gather x1, waiting for transfers between devices, shards(): values = lax.all_gather(value_b, 'gx', axis=0, tiled=True)  71.5 us
    psum x1, waiting for transfers between devices, shards(): lax.psum(partial_out.astype(jnp.bfloat16), 'gy').astype(jnp.float32)  68 us
    psum x1, blocking collectives, shards(): low = lax.psum(partial_low.astype(jnp.bfloat16), 'gy')  61.6 us
    psum x1, blocking collectives, shards(): lax.psum((jnp.sum(query * query, axis=(1, 2)), jnp.sum(key_raw * key_raw,...  28.5 us
    dot_general x16, matrix products, attend(): jnp.einsum('htk,khe->hte', weights.astype(jnp.bfloat16), values, preferre...  21.9 us
    dot_general x16, matrix products, attend(): jnp.einsum('the,khe->htk', query_b, key_vectors, preferred_element_type=j...  19 us
    all_to_all x1, waiting for transfers between devices, shards(): lax.all_to_all(pages[order], 'gx', split_axis=0, concat_axis=0, tiled=True)  13.8 us
  transfers between devices with their start and end apart: 5, of which 5 were waited for; matrix products, arithmetic and copies ran while one was open for 2% of the time, Pallas kernels for 0%

commit v1 on v0

v1 whole, which is shorter than its diff:
```python
import jax
import jax.numpy as jnp
from jax import lax
from jax.experimental import pallas as pl
from jax.experimental.pallas import tpu as pltpu
from jax.sharding import PartitionSpec as P

MODEL_WIDTH = 2048
HEADS = 16
HEAD = 128
RANK = 16
PAGE = 8
REQS = 4
ROWS = 256
CHIP_ROWS = 2 * ROWS
GROUPS = 32
PAGES_HERE = ROWS // PAGE
HOPS = 4
FAR = 5
CHIPS = GROUPS // 2
NEG = -1e30
FLOOR = -1e29
BIG = 1 << 30
SCORE_SCALE = 1.4426950408889634 * HEAD ** (-0.5)
F32 = jnp.float32
BF16 = jnp.bfloat16

VMEM = pl.BlockSpec(memory_space=pltpu.VMEM)
SMEM = pl.BlockSpec(memory_space=pltpu.SMEM)


def contract(a, b, dims, precision=None):
    return lax.dot_general(
        a, b, (((dims[0],), (dims[1],)), ((), ())), precision=precision, preferred_element_type=F32
    )


def chips_apart(distance):
    return [(i, i + 2 * distance) for i in range(GROUPS) if 0 <= i + 2 * distance < GROUPS]


SIBLING = [(i, i ^ 1) for i in range(GROUPS)]


def low_kernel(lengths, adapters, storage, tokens, down, out):
    rows = lax.axis_index("gx") * ROWS + lax.broadcasted_iota(jnp.int32, (1, ROWS), 1)
    member = lax.axis_index("gy")
    begin = jnp.int32(0)
    chosen = jnp.zeros((1, ROWS), F32)
    for r in range(REQS):
        end = begin + lengths[r]
        from_row = jnp.where(storage[adapters[r]] == member, begin, BIG)
        chosen = jnp.where((rows >= from_row) & (rows < end), 1.0, chosen)
        begin = end
    reduced = contract(down[...], tokens[...], (1, 1))
    low = jnp.where(chosen > 0.0, reduced, 0.0).astype(BF16)
    for j in range(HEADS):
        out[j] = low


def project_kernel(lengths, adapters, storage, base, lows, up, qkv, squares):
    rows = lax.axis_index("gx") * ROWS + lax.broadcasted_iota(jnp.int32, (1, ROWS), 1)
    low = lows[0].astype(F32)
    for j in range(1, HEADS):
        low = low + lows[j].astype(F32)
    inside = []
    slots = []
    begin = jnp.int32(0)
    for r in range(REQS):
        end = begin + lengths[r]
        inside.append((rows >= begin) & (rows < end))
        slots.append(storage[adapters[r]])
        begin = end
    ones = jnp.ones((8, HEAD), F32)
    totals = []
    for c in range(3):
        part = low[c * RANK : (c + 1) * RANK]
        spread = jnp.concatenate([jnp.where(hit, part, 0.0) for hit in inside], axis=0).astype(BF16)
        maps = jnp.concatenate([up[slot, c] for slot in slots], axis=0)
        cols = slice(c * HEAD, (c + 1) * HEAD)
        value = base[:, cols] + contract(spread, maps, (0, 0))
        qkv[:, cols] = value
        if c < 2:
            totals.append(contract(ones, value * value, (1, 1), lax.Precision.HIGHEST))
    line = lax.broadcasted_iota(jnp.int32, (8, ROWS), 0)
    both = jnp.where(line < 4, totals[0], totals[1])
    for j in range(HEADS):
        squares[j] = both


def rotate_kernel(qkv, squares, query_gain, key_gain, cosine, sine, query, keys_values):
    total = squares[0]
    for j in range(1, HEADS):
        total = total + squares[j]
    line = lax.broadcasted_iota(jnp.int32, (8, HEAD), 0)

    def rotated(cols, pick, gain):
        square = contract(total, jnp.where(line == pick, 1.0, 0.0), (0, 0), lax.Precision.HIGHEST)
        value = qkv[:, cols] * lax.rsqrt(square / MODEL_WIDTH + 1e-06) * gain[...]
        return value * cosine[...] + pltpu.roll(value, HEAD // 2, 1) * sine[...]

    query[...] = (rotated(slice(0, HEAD), 0, query_gain) * SCORE_SCALE).astype(BF16)
    keys_values[0:ROWS] = rotated(slice(HEAD, 2 * HEAD), 4, key_gain).astype(BF16)
    keys_values[ROWS : 2 * ROWS] = qkv[:, 2 * HEAD : 3 * HEAD].astype(BF16)


def attend(lengths, query, blocks, scores, query_chip, key_chip):
    core = lax.rem(lax.axis_index("gx"), 2)
    lane = lax.broadcasted_iota(jnp.int32, (1, CHIP_ROWS), 1)
    flip = jnp.where(lane < ROWS, lane, lane - CHIP_ROWS)
    rows = query_chip * CHIP_ROWS + jnp.where(core == 0, lane, flip + ROWS)
    begin = jnp.zeros((1, CHIP_ROWS), jnp.int32)
    run = jnp.int32(0)
    for r in range(REQS - 1):
        run = run + lengths[r]
        begin = jnp.where(rows >= run, run, begin)
    place = lax.broadcasted_iota(jnp.int32, (ROWS, CHIP_ROWS), 0)
    best = jnp.full((1, CHIP_ROWS), FLOOR, F32)
    for i, block in enumerate(blocks):
        first = (key_chip - i) * CHIP_ROWS + core * ROWS
        score = contract(block[0:ROWS], query, (1, 1))
        allowed = (place >= begin - first) & (place <= rows - first)
        score = jnp.where(allowed, score, NEG)
        scores[i] = score
        best = jnp.maximum(best, jnp.max(score, axis=0, keepdims=True))
    best = best.astype(BF16).astype(F32)
    total = jnp.zeros((1, CHIP_ROWS), F32)
    accum = jnp.zeros((HEAD, CHIP_ROWS), F32)
    for i, block in enumerate(blocks):
        weight = jnp.exp2(scores[i] - best)
        total = total + jnp.sum(weight, axis=0, keepdims=True)
        accum = accum + contract(block[ROWS : 2 * ROWS], weight.astype(BF16), (0, 0))
    return best, total, accum


def far_kernel(lengths, query, b0, b1, b2, b3, out, scores):
    chip = lax.axis_index("gx") // 2
    best, total, accum = attend(
        lengths, query[...], (b0, b1, b2, b3), scores, chip + FAR, chip
    )
    out[0:HEAD] = accum.astype(BF16)
    line = lax.broadcasted_iota(jnp.int32, (16, CHIP_ROWS), 0)
    high = total.astype(BF16).astype(F32)
    rest = jnp.where(line == 1, high, jnp.where(line == 2, total - high, 0.0))
    out[HEAD : HEAD + 16] = jnp.where(line == 0, best, rest).astype(BF16)


def near_kernel(lengths, query, b0, b1, b2, b3, b4, out, scores):
    chip = lax.axis_index("gx") // 2
    best, total, accum = attend(
        lengths, query[...], (b0, b1, b2, b3, b4), scores, chip, chip
    )
    out[0:HEAD] = accum
    line = lax.broadcasted_iota(jnp.int32, (8, CHIP_ROWS), 0)
    out[HEAD : HEAD + 8] = jnp.where(line == 0, best, total)


def merge_kernel(near, far, mine, theirs):
    chip = lax.axis_index("gx") // 2
    stats = far[HEAD : HEAD + 16].astype(F32)
    best_far = jnp.where(chip >= FAR, stats[0:1], FLOOR)
    total_far = stats[1:2] + stats[2:3]
    tail = near[HEAD : HEAD + 8]
    best_near = tail[0:1]
    best = jnp.maximum(best_near, best_far)
    a = jnp.exp2(best_near - best)
    b = jnp.exp2(best_far - best)
    accum = near[0:HEAD] * a + far[0:HEAD].astype(F32) * b
    total = tail[1:2] * a + total_far * b
    line = lax.broadcasted_iota(jnp.int32, (8, CHIP_ROWS), 0)
    stat = jnp.where(line == 0, best, total)
    mine[0:HEAD] = accum[:, 0:ROWS]
    mine[HEAD : HEAD + 8] = stat[:, 0:ROWS]
    theirs[0:HEAD] = accum[:, ROWS:CHIP_ROWS]
    theirs[HEAD : HEAD + 8] = stat[:, ROWS:CHIP_ROWS]


def finish_kernel(mine, other, out):
    s0 = mine[HEAD : HEAD + 8]
    s1 = other[HEAD : HEAD + 8]
    best = jnp.maximum(s0[0:1], s1[0:1])
    a = jnp.exp2(s0[0:1] - best)
    b = jnp.exp2(s1[0:1] - best)
    total = s0[1:2] * a + s1[1:2] * b
    attn = (mine[0:HEAD] * a + other[0:HEAD] * b) / total
    attn = attn.T.astype(BF16)
    for j in range(HEADS):
        out[j] = attn


TILE = 512


def output_kernel(attn, weight, tokens, gain, out, rows_attn, result, square):
    step = pl.program_id(0)

    @pl.when(step == 0)
    def _():
        for h in range(HEADS):
            rows_attn[:, h * HEAD : (h + 1) * HEAD] = attn[h]
        square[...] = jnp.zeros_like(square)

    part = jnp.dot(rows_attn[...], weight[...], preferred_element_type=F32)
    result[step] = part
    square[...] += jnp.sum(part * part, axis=1, keepdims=True)

    @pl.when(step == pl.num_programs(0) - 1)
    def _():
        scale = lax.rsqrt(square[...] / MODEL_WIDTH + 1e-06)
        for s in range(MODEL_WIDTH // TILE):
            cols = slice(s * TILE, (s + 1) * TILE)
            normed = result[s] * scale * gain[:, cols]
            out[:, cols] = (tokens[:, cols].astype(F32) + normed).astype(BF16)


def project_out(attn, weight, tokens, gain):
    whole = lambda shape: pl.BlockSpec(shape, lambda n: (0,) * len(shape))
    return pl.pallas_call(
        output_kernel,
        grid=(MODEL_WIDTH // TILE,),
        in_specs=[
            whole((HEADS, ROWS, HEAD)),
            pl.BlockSpec((MODEL_WIDTH, TILE), lambda n: (0, n)),
            whole((ROWS, MODEL_WIDTH)),
            whole((1, MODEL_WIDTH)),
        ],
        out_specs=whole((ROWS, MODEL_WIDTH)),
        out_shape=jax.ShapeDtypeStruct((ROWS, MODEL_WIDTH), BF16),
        scratch_shapes=[
            pltpu.VMEM((ROWS, MODEL_WIDTH), BF16),
            pltpu.VMEM((MODEL_WIDTH // TILE, ROWS, TILE), F32),
            pltpu.VMEM((ROWS, 1), F32),
        ],
        name="project_out",
    )(attn, weight, tokens, gain)


def local(kernel, name, scalars, arrays, outs, scratch=()):
    specs = [SMEM] * len(scalars) + [VMEM] * len(arrays)
    shapes = [jax.ShapeDtypeStruct(shape, dtype) for shape, dtype in outs]
    single = len(shapes) == 1
    return pl.pallas_call(
        kernel,
        in_specs=specs,
        out_specs=VMEM if single else [VMEM] * len(shapes),
        out_shape=shapes[0] if single else shapes,
        scratch_shapes=list(scratch),
        name=name,
    )(*scalars, *arrays)


def exchange(copies):
    return lax.all_to_all(copies, "gy", split_axis=0, concat_axis=0, tiled=True)


def angles(lengths):
    rows = lax.axis_index("gx") * ROWS + jnp.arange(ROWS)
    begin = jnp.zeros((ROWS,), jnp.int32)
    run = jnp.int32(0)
    for r in range(REQS - 1):
        run = run + lengths[r]
        begin = jnp.where(rows >= run, run, begin)
    half = HEAD // 2
    freq = 500000.0 ** (-(jnp.arange(half).astype(F32) * 2.0) / HEAD)
    angle = (rows - begin).astype(F32)[:, None] * freq[None, :]
    cosine = jnp.cos(angle)
    sine = jnp.sin(angle)
    return jnp.concatenate([cosine, cosine], axis=1), jnp.concatenate([-sine, sine], axis=1)


def store_pages(keys_values, page_cache_slot):
    token = jnp.arange(ROWS)
    slot_of_token = jnp.repeat(page_cache_slot, PAGE)
    owner = slot_of_token // PAGES_HERE
    inner = (slot_of_token % PAGES_HERE).astype(BF16)
    goes_to = owner * PAGE + token % PAGE
    pick = (goes_to[None, :] == token[:, None]).astype(BF16)
    block = jnp.concatenate(
        [
            keys_values[0:ROWS],
            keys_values[ROWS : 2 * ROWS],
            jnp.broadcast_to(inner[:, None], (ROWS, HEAD)),
        ],
        axis=1,
    )
    sent = jnp.dot(pick, block, preferred_element_type=F32).astype(BF16)
    got = lax.all_to_all(
        sent.reshape(GROUPS, PAGE, 3 * HEAD), "gx", split_axis=0, concat_axis=0, tiled=True
    ).reshape(ROWS, 3 * HEAD)
    place = got[:, 2 * HEAD].astype(jnp.int32) * PAGE + token % PAGE
    put = (place[:, None] == token[None, :]).astype(BF16)
    stored = contract(put, got[:, 0 : 2 * HEAD], (0, 0)).astype(BF16)
    return stored.reshape(PAGES_HERE, PAGE, 1, 2 * HEAD)


def shards(
    tokens,
    lengths,
    adapter_of_request,
    adapter_storage_slot,
    page_cache_slot,
    query_key_value_weight,
    adapter_down_maps,
    adapter_up_maps,
    query_norm_gain,
    key_norm_gain,
    output_weight,
    post_norm_gain,
):
    whole_weight = lax.all_gather(output_weight[0], "gy", axis=0, tiled=True)
    scalars = (lengths, adapter_of_request, adapter_storage_slot)
    lows = local(
        low_kernel,
        "low",
        scalars,
        (tokens, jnp.swapaxes(adapter_down_maps[0], 0, 1)),
        [((HEADS, 3 * RANK, ROWS), BF16)],
    )
    lows = exchange(lows)
    base = jnp.dot(tokens, query_key_value_weight[:, 0], preferred_element_type=F32)
    cosine, sine = angles(lengths)
    qkv, squares = local(
        project_kernel,
        "project",
        scalars,
        (base, lows, adapter_up_maps[:, :, :, 0]),
        [((ROWS, 3 * HEAD), F32), ((HEADS, 8, ROWS), F32)],
    )
    squares = exchange(squares)
    query, block = local(
        rotate_kernel,
        "rotate",
        (),
        (qkv, squares, query_norm_gain, key_norm_gain, cosine, sine),
        [((ROWS, HEAD), BF16), ((2 * ROWS, HEAD), BF16)],
    )
    blocks = [block]
    for _ in range(HOPS):
        blocks.append(lax.ppermute(blocks[-1], "gx", chips_apart(1)))
    sibling = lax.ppermute(query, "gx", SIBLING)
    queries = jnp.concatenate([query, sibling], axis=0)
    far_queries = lax.ppermute(queries, "gx", chips_apart(-FAR))
    far = local(
        far_kernel,
        "attend_far",
        (lengths,),
        (far_queries, *blocks[:HOPS]),
        [((HEAD + 16, CHIP_ROWS), BF16)],
        [pltpu.VMEM((HOPS, ROWS, CHIP_ROWS), F32)],
    )
    far = lax.ppermute(far, "gx", chips_apart(FAR))
    near = local(
        near_kernel,
        "attend_near",
        (lengths,),
        (queries, *blocks),
        [((HEAD + 8, CHIP_ROWS), F32)],
        [pltpu.VMEM((HOPS + 1, ROWS, CHIP_ROWS), F32)],
    )
    mine, theirs = local(
        merge_kernel,
        "merge",
        (),
        (near, far),
        [((HEAD + 8, ROWS), F32), ((HEAD + 8, ROWS), F32)],
    )
    other = lax.ppermute(theirs, "gx", SIBLING)
    attn = local(finish_kernel, "finish", (), (mine, other), [((HEADS, ROWS, HEAD), BF16)])
    attn = exchange(attn)
    mixed = project_out(attn, whole_weight, tokens, post_norm_gain[None, :])
    kv_cache = store_pages(block, page_cache_slot)
    return (mixed, kv_cache)


def solution(mesh):
    return jax.shard_map(
        shards,
        mesh=mesh,
        in_specs=(
            P("gx", None),
            P(),
            P(),
            P(),
            P("gx"),
            P(None, "gy", None),
            P("gy", None, None),
            P(None, None, None, "gy", None),
            P("gy", None),
            P("gy", None),
            P("gy", None, None),
            P(),
        ),
        out_specs=(P("gx", None), P("gx", None, "gy", None)),
        check_vma=False,
    )
```

time: 446 us -> 168 us (0.38)
  waiting for transfers between devices: 257 us -> 43.2 us
  blocking collectives: 90.1 us -> 0 us
  starting transfers between devices: 12.8 us -> 67.5 us
  matrix products: 46.3 us -> 3.37 us
  Pallas kernels: 0 us -> 25.8 us
  other arithmetic: 19.1 us -> 2.13 us
    all_gather x2 -> x1, waiting for transfers between devices: 165 us -> 0.01 us  [shards(): whole_weight = lax.all_gather(output_weight[0], 'gy', axis=0, tiled=True)]
    psum x2 -> x0, blocking collectives: 90.1 us -> none  [the longest x1 61.6 us: shards(): low = lax.psum(partial_low.astype(jnp.bfloat16), 'gy')]
    psum x1 -> x0, waiting for transfers between devices: 68 us -> none  [shards(): lax.psum(partial_out.astype(jnp.bfloat16), 'gy').astype(jnp.float32)]
    dot_general x36 -> x3, matrix products: 46.3 us -> 3.37 us  [the longest x1 1.46 us: shards(): jnp.dot(tokens, query_key_value_weight[:, 0], preferred_element_type=F32)]
    ppermute x0 -> x8, starting transfers between devices: none -> 34.6 us  [the longest x4 14.9 us: shards(): blocks.append(lax.ppermute(blocks[-1], 'gx', chips_apart(1)))]
    pallas_call x0 -> x8, Pallas kernels: none -> 25.8 us  [the longest x7 17.9 us: local(): pl.pallas_call(kernel, in_specs=specs, out_specs=VMEM if single else [VME...]
    all_to_all x2 -> x4, starting transfers between devices: 12.7 us -> 32.9 us  [the longest x1 17.8 us: store_pages(): lax.all_to_all(sent.reshape(GROUPS, PAGE, 3 * HEAD), 'gx', split_axis=0,...]
    ppermute x0 -> x8, waiting for transfers between devices: none -> 17.7 us  [the longest x1 8.8 us: shards(): far_queries = lax.ppermute(queries, 'gx', chips_apart(-FAR))]
  transfers between devices with their start and end apart: 5 -> 13, of which waited for: 5 -> 7; matrix products, arithmetic and copies ran while one was open for 2% -> 5% of each run, Pallas kernels for 0% -> 11%
where the time goes in v1:
time: 168 us; the launch traced here: 167 us
  starting transfers between devices  67.5 us (40%)
  waiting for transfers between devices  43.2 us (26%)
  Pallas kernels  25.8 us (15%)
  between operations  16.2 us (10%)
  local copies, waits for them, and re-layouts  8.33 us (5%)
  matrix products  3.37 us (2%)
  other arithmetic  2.13 us (1%)
    all_to_all x3, waiting for transfers between devices, exchange(): return lax.all_to_all(copies, 'gy', split_axis=0, concat_axis=0, tiled=True)  24.8 us
    pallas_call x7, Pallas kernels, local(): pl.pallas_call(kernel, in_specs=specs, out_specs=VMEM if single else [VME...  17.9 us
    all_to_all x1, starting transfers between devices, store_pages(): lax.all_to_all(sent.reshape(GROUPS, PAGE, 3 * HEAD), 'gx', split_axis=0,...  17.8 us
    all_to_all x3, starting transfers between devices, exchange(): return lax.all_to_all(copies, 'gy', split_axis=0, concat_axis=0, tiled=True)  15.1 us
    ppermute x4, starting transfers between devices, shards(): blocks.append(lax.ppermute(blocks[-1], 'gx', chips_apart(1)))  14.9 us
    ppermute x1, starting transfers between devices, shards(): other = lax.ppermute(theirs, 'gx', SIBLING)  13.2 us
    ppermute x1, waiting for transfers between devices, shards(): far_queries = lax.ppermute(queries, 'gx', chips_apart(-FAR))  8.8 us
    pallas_call x1, Pallas kernels, project_out(): pl.pallas_call(output_kernel, grid=(MODEL_WIDTH // TILE,), in_specs=[whol...  7.98 us
  transfers between devices with their start and end apart: 13, of which 7 were waited for; matrix products, arithmetic and copies ran while one was open for 5% of the time, Pallas kernels for 11%

profile of v1, /device:TPU:1, one launch (start us, length us, event | category | flops | bytes accessed | tf_op | source)
XLA Modules:
  0.0 166.6 jit_solution(17159066712048440701)
XLA Ops:
  7.2 0.7 all-gather.3.cloned.1.call-update
  7.9 2.6 %low.1 = bf16[16,48,256]{2,1,0:T(8,128)(2,1)} custom-call(s32[4]{0:T(128)} %lengths.7, s32[4]{0:T(128)} %adapters.3, s32[16]{0:T(128)} %storage.3, bf16[256,2048]{1,0:T(8,128)(2,1)} %tokens.3, bf16[48,2048]{1,0:T(8,128)(2,1)} %bitcast.24), custom_call_target="tpu_custom_call" | custom-call | tf_op jit(solution)/shard_map/low/pallas_call | solution.py:242
  10.5 7.6 %all-to-all-start = ((bf16[16,48,256]{2,1,0:T(8,128)(2,1)}), bf16[16,48,256]{2,1,0:T(8,128)(2,1)S(1)}, u32[]{:S(2)}, u32[]{:S(2)}) async-start(bf16[16,48,256]{2,1,0:T(8,128)(2,1)} %low.1), calls=%async_computation | async-start | bytes 786432 | tf_op jit(solution)/shard_map/all_to_all | solution.py:253
  18.1 0.6 fusion.24
  20.7 0.6 fusion.20
  21.4 0.5 fusion.17
  22.0 0.1 reshape.119
  22.1 1.5 fusion.base
  23.6 2.8 %all-to-all-done.lows = bf16[16,48,256]{2,1,0:T(8,128)(2,1)S(1)} async-done(((bf16[16,48,256]{2,1,0:T(8,128)(2,1)}), bf16[16,48,256]{2,1,0:T(8,128)(2,1)S(1)}, u32[]{:S(2)}, u32[]{:S(2)}) %all-to-all-start) | async-done | bytes 393248 | tf_op jit(solution)/shard_map/all_to_all | solution.py:253
  26.4 0.7 copy-done.3
  27.1 2.6 %project.1 = (f32[256,384]{1,0:T(8,128)}, f32[16,8,256]{2,1,0:T(8,128)}) custom-call(s32[4]{0:T(128)} %lengths.7, s32[4]{0:T(128)} %adapters.3, s32[16]{0:T(128)} %storage.3, f32[256,384]{1,0:T(8,128)} %fusion.base, bf16[16,48,256]{2,1,0:T(8,128)(2,1)} %copy-done.3, bf16[16,3,16,128]{3,2,1,0:T(8,128)(2,1)} %bitcast.23), custom_call_target="tpu_custom_call" | custom-call | tf_op jit(solution)/shard_map/project/pallas_call | solution.py:242
  29.7 3.8 %all-to-all-start.1 = ((f32[16,8,256]{2,1,0:T(8,128)}), f32[16,8,256]{2,1,0:T(8,128)S(1)}, u32[]{:S(2)}, u32[]{:S(2)}) async-start(f32[16,8,256]{2,1,0:T(8,128)} %get-tuple-element.9), calls=%async_computation.1 | async-start | bytes 262144 | tf_op jit(solution)/shard_map/all_to_all | solution.py:253
  33.6 0.8 pad_maximum_fusion
  34.4 6.0 %all-to-all-done.1.squares = f32[16,8,256]{2,1,0:T(8,128)S(1)} async-done(((f32[16,8,256]{2,1,0:T(8,128)}), f32[16,8,256]{2,1,0:T(8,128)S(1)}, u32[]{:S(2)}, u32[]{:S(2)}) %all-to-all-start.1) | async-done | bytes 131104 | tf_op jit(solution)/shard_map/all_to_all | solution.py:253
  40.4 0.7 copy-done.4
  41.0 2.4 %rotate.1 = (bf16[256,128]{1,0:T(8,128)(2,1)}, bf16[512,128]{1,0:T(8,128)(2,1)}) custom-call(f32[256,384]{1,0:T(8,128)} %get-tuple-element.8.qkv, f32[16,8,256]{2,1,0:T(8,128)} %copy-done.4, f32[1,128]{1,0:T(1,128)} %query_gain.1, f32[1,128]{1,0:T(1,128)} %key_gain.1, f32[256,128]{1,0:T(8,128)} %get-tuple-element.30.cosine, f32[256,128]{1,0:T(8,128)} %get-tuple-element.31.sine), custom_call_target="tpu_custom_call" | custom-call | tf_op jit(solution)/shard_map/rotate/pallas_call | solution.py:242
  43.5 5.3 %collective-permute-start.1 = (bf16[512,128]{1,0:T(8,128)(2,1)}, bf16[512,128]{1,0:T(8,128)(2,1)S(1)}, u32[]{:S(2)}, u32[]{:S(2)}) collective-permute-start(bf16[512,128]{1,0:T(8,128)(2,1)} %get-tuple-element.11.b0), channel_id=1, source_target_pairs={{0,32},{16,48},{32,64},{48,80},{64,96},{80,112},{96,128},{112,144}... | collective-permute-start | bytes 393224 | tf_op jit(solution)/shard_map/ppermute | solution.py:339
  48.8 0.9 fusion.23
  49.7 0.1 broadcast_in_dim.30
  49.8 0.9 fusion.2
  50.8 17.8 %all-to-all-start.3 = ((bf16[32,8,384]{2,1,0:T(8,128)(2,1)}), bf16[32,8,384]{2,1,0:T(8,128)(2,1)S(1)}, u32[]{:S(2)}, u32[]{:S(2)}) async-start(bf16[32,8,384]{2,1,0:T(8,128)(2,1)} %fusion.2), calls=%async_computation.3 | async-start | bytes 393216 | tf_op jit(solution)/shard_map/all_to_all | solution.py:287
  68.6 2.1 %collective-permute-start = (bf16[256,128]{1,0:T(8,128)(2,1)}, bf16[256,128]{1,0:T(8,128)(2,1)S(1)}, u32[]{:S(2)}, u32[]{:S(2)}) collective-permute-start(bf16[256,128]{1,0:T(8,128)(2,1)} %get-tuple-element.10), channel_id=1, source_target_pairs={{0,16},{16,0},{32,48},{48,32},{64,80},{80,64},{96,112},{112,96},{1... | collective-permute-start | bytes 196616 | tf_op jit(solution)/shard_map/ppermute | solution.py:340
  70.8 3.4 %collective-permute-start.2 = (bf16[512,128]{1,0:T(8,128)(2,1)S(1)}, bf16[512,128]{1,0:T(8,128)(2,1)S(1)}, u32[]{:S(2)}, u32[]{:S(2)}) collective-permute-start(bf16[512,128]{1,0:T(8,128)(2,1)S(1)} %collective-permute-done.1.b1), channel_id=1, source_target_pairs={{0,32},{16,48},{32,64},{48,80},{64,96},{80,112},{96,128},{112,144}... | collective-permute-start | bytes 393224 | tf_op jit(solution)/shard_map/ppermute | solution.py:339
  74.2 0.8 constant_dynamic-update-slice_fusion.1
  75.1 1.3 collective-permute-start.5
  76.4 4.2 %collective-permute-done.2.b2 = bf16[512,128]{1,0:T(8,128)(2,1)S(1)} collective-permute-done((bf16[512,128]{1,0:T(8,128)(2,1)S(1)}, bf16[512,128]{1,0:T(8,128)(2,1)S(1)}, u32[]{:S(2)}, u32[]{:S(2)}) %collective-permute-start.2) | collective-permute-done | bytes 131104 | tf_op jit(solution)/shard_map/ppermute | solution.py:339
  80.6 4.4 %collective-permute-start.3 = (bf16[512,128]{1,0:T(8,128)(2,1)S(1)}, bf16[512,128]{1,0:T(8,128)(2,1)S(1)}, u32[]{:S(2)}, u32[]{:S(2)}) collective-permute-start(bf16[512,128]{1,0:T(8,128)(2,1)S(1)} %collective-permute-done.2.b2), channel_id=1, source_target_pairs={{0,32},{16,48},{32,64},{48,80},{64,96},{80,112},{96,128},{112,144}... | collective-permute-start | bytes 393224 | tf_op jit(solution)/shard_map/ppermute | solution.py:339
  84.9 8.8 %collective-permute-done.5.query = bf16[512,128]{1,0:T(8,128)(2,1)S(1)} collective-permute-done((bf16[512,128]{1,0:T(8,128)(2,1)S(1)}, bf16[512,128]{1,0:T(8,128)(2,1)S(1)}, u32[]{:S(2)}, u32[]{:S(2)}) %collective-permute-start.5) | collective-permute-done | bytes 131104 | tf_op jit(solution)/shard_map/ppermute | solution.py:342
  93.7 0.6 copy-done.11
  94.4 0.6 copy-done.7
  95.0 3.0 %attend_far.1 = bf16[144,512]{1,0:T(8,128)(2,1)} custom-call(s32[4]{0:T(128)} %lengths.7, bf16[512,128]{1,0:T(8,128)(2,1)} %copy-done.11, bf16[512,128]{1,0:T(8,128)(2,1)} %get-tuple-element.11.b0, bf16[512,128]{1,0:T(8,128)(2,1)} %copy-done.5, bf16[512,128]{1,0:T(8,128)(2,1)} %copy-done.6, bf16[512,128]{1,0:T(8,128)(2,1)} %copy-done.7), custom_call_target="tpu_custom_call" | custom-call | tf_op jit(solution)/shard_map/attend_far/pallas_call | solution.py:242
  98.0 3.0 %collective-permute-start.6 = (bf16[144,512]{1,0:T(8,128)(2,1)}, bf16[144,512]{1,0:T(8,128)(2,1)S(1)}, u32[]{:S(2)}, u32[]{:S(2)}) collective-permute-start(bf16[144,512]{1,0:T(8,128)(2,1)} %attend_far.1), channel_id=1, source_target_pairs={{0,160},{16,176},{32,192},{48,208},{64,224},{80,240},{96,256},{112... | collective-permute-start | bytes 442376 | tf_op jit(solution)/shard_map/ppermute | solution.py:351
  101.1 1.8 %collective-permute-start.4 = (bf16[512,128]{1,0:T(8,128)(2,1)}, bf16[512,128]{1,0:T(8,128)(2,1)S(1)}, u32[]{:S(2)}, u32[]{:S(2)}) collective-permute-start(bf16[512,128]{1,0:T(8,128)(2,1)} %copy-done.7), channel_id=1, source_target_pairs={{0,32},{16,48},{32,64},{48,80},{64,96},{80,112},{96,128},{112,144}... | collective-permute-start | bytes 393224 | tf_op jit(solution)/shard_map/ppermute | solution.py:339
  102.9 3.5 %collective-permute-done.4.b4 = bf16[512,128]{1,0:T(8,128)(2,1)S(1)} collective-permute-done((bf16[512,128]{1,0:T(8,128)(2,1)}, bf16[512,128]{1,0:T(8,128)(2,1)S(1)}, u32[]{:S(2)}, u32[]{:S(2)}) %collective-permute-start.4) | collective-permute-done | bytes 131104 | tf_op jit(solution)/shard_map/ppermute | solution.py:339
  106.4 0.6 copy-done.12
  107.0 3.3 %attend_near.1.near = f32[136,512]{1,0:T(8,128)} custom-call(s32[4]{0:T(128)} %lengths.7, bf16[512,128]{1,0:T(8,128)(2,1)} %copy-done.8, bf16[512,128]{1,0:T(8,128)(2,1)} %get-tuple-element.11.b0, bf16[512,128]{1,0:T(8,128)(2,1)} %copy-done.5, bf16[512,128]{1,0:T(8,128)(2,1)} %copy-done.6, bf16[512,128]{1,0:T(8,128)(2,1)} %copy-done.7, ...), custom_call_target="tpu_custom_call" | custom-call | tf_op jit(solution)/shard_map/attend_near/pallas_call | solution.py:242
  110.4 0.7 copy-done.9
  111.0 1.8 %merge.1 = (f32[136,256]{1,0:T(8,128)}, f32[136,256]{1,0:T(8,128)}) custom-call(f32[136,512]{1,0:T(8,128)} %attend_near.1.near, bf16[144,512]{1,0:T(8,128)(2,1)} %copy-done.9), custom_call_target="tpu_custom_call" | custom-call | tf_op jit(solution)/shard_map/merge/pallas_call | solution.py:242
  112.8 13.2 %collective-permute-start.7 = (f32[136,256]{1,0:T(8,128)}, f32[136,256]{1,0:T(8,128)S(1)}, u32[]{:S(2)}, u32[]{:S(2)}) collective-permute-start(f32[136,256]{1,0:T(8,128)} %get-tuple-element.13), channel_id=1, source_target_pairs={{0,16},{16,0},{32,48},{48,32},{64,80},{80,64},{96,112},{112,96},{1... | collective-permute-start | bytes 417800 | tf_op jit(solution)/shard_map/ppermute | solution.py:367
  126.0 1.2 collective-permute-done.7.other
  127.2 0.7 copy-done.10
  127.9 2.2 %finish.1 = bf16[16,256,128]{2,1,0:T(8,128)(2,1)} custom-call(f32[136,256]{1,0:T(8,128)} %get-tuple-element.12.mine, f32[136,256]{1,0:T(8,128)} %copy-done.10), custom_call_target="tpu_custom_call" | custom-call | tf_op jit(solution)/shard_map/finish/pallas_call | solution.py:242
  130.0 3.7 %all-to-all-start.2 = ((bf16[16,256,128]{2,1,0:T(8,128)(2,1)}), bf16[16,256,128]{2,1,0:T(8,128)(2,1)S(1)}, u32[]{:S(2)}, u32[]{:S(2)}) async-start(bf16[16,256,128]{2,1,0:T(8,128)(2,1)} %finish.1), calls=%async_computation.2 | async-start | bytes 2097152 | tf_op jit(solution)/shard_map/all_to_all | solution.py:253
  133.7 0.1 fusion.10
  133.8 1.0 fusion.3
  134.8 16.0 %all-to-all-done.2.attn = bf16[16,256,128]{2,1,0:T(8,128)(2,1)S(1)} async-done(((bf16[16,256,128]{2,1,0:T(8,128)(2,1)}), bf16[16,256,128]{2,1,0:T(8,128)(2,1)S(1)}, u32[]{:S(2)}, u32[]{:S(2)}) %all-to-all-start.2) | async-done | bytes 1048608 | tf_op jit(solution)/shard_map/all_to_all | solution.py:253
  150.8 1.0 copy-done.2
  151.8 8.0 %project_out.1 = bf16[256,2048]{1,0:T(8,128)(2,1)} custom-call(bf16[16,256,128]{2,1,0:T(8,128)(2,1)} %copy-done.2, bf16[2048,2048]{1,0:T(8,128)(2,1)} %bitcast.20, bf16[256,2048]{1,0:T(8,128)(2,1)} %tokens.3, f32[1,2048]{1,0:T(1,128)} %bitcast.25), custom_call_target="tpu_custom_call" | custom-call | tf_op jit(solution)/shard_map/project_out/pallas_call | solution.py:218
  (33 shorter events, 0.2 us)
Async XLA Ops:
  7.2 14.9 %copy-start = (bf16[2048,1,384]{2,0,1:T(8,128)(2,1)S(1)}, bf16[2048,1,384]{2,0,1:T(8,128)(2,1)}, u32[]{:S(2)}) copy-start(bf16[2048,1,384]{2,0,1:T(8,128)(2,1)} %param.17) | copy-start | bytes 4718596
  7.2 11.0 %copy-start.13 = (s32[4]{0:T(128)S(1)}, s32[4]{0:T(128)}, u32[]{:S(2)}) copy-start(s32[4]{0:T(128)} %lengths.7) | copy-start | bytes 52
  7.2 14.7 %copy-start.14 = (s32[32]{0:T(128)S(1)}, s32[32]{0:T(128)}, u32[]{:S(2)}) copy-start(s32[32]{0:T(128)} %param.16) | copy-start | bytes 388
  7.2 143.6 %all-gather.3.cloned.1.call-start = ((), (), s32[]{:S(2)}) async-start(), calls=%async_computation.4 | async-start | bytes 8912896 | tf_op jit(solution)/shard_map/all_gather | solution.py:310
  7.9 14.2 %copy-start.1 = (bf16[256,2048]{1,0:T(8,128)(2,1)S(1)}, bf16[256,2048]{1,0:T(8,128)(2,1)}, u32[]{:S(2)}) copy-start(bf16[256,2048]{1,0:T(8,128)(2,1)} %tokens.3) | copy-start | bytes 3145732
  10.5 15.8 %all-to-all-start = ((bf16[16,48,256]{2,1,0:T(8,128)(2,1)}), bf16[16,48,256]{2,1,0:T(8,128)(2,1)S(1)}, u32[]{:S(2)}, u32[]{:S(2)}) async-start(bf16[16,48,256]{2,1,0:T(8,128)(2,1)} %low.1), calls=%async_computation | async-start | bytes 786432 | tf_op jit(solution)/shard_map/all_to_all | solution.py:253
  26.4 0.7 copy-start.3
  29.7 10.7 %all-to-all-start.1 = ((f32[16,8,256]{2,1,0:T(8,128)}), f32[16,8,256]{2,1,0:T(8,128)S(1)}, u32[]{:S(2)}, u32[]{:S(2)}) async-start(f32[16,8,256]{2,1,0:T(8,128)} %get-tuple-element.9), calls=%async_computation.1 | async-start | bytes 262144 | tf_op jit(solution)/shard_map/all_to_all | solution.py:253
  40.4 0.7 copy-start.4
  43.5 27.3 %collective-permute-start.1 = (bf16[512,128]{1,0:T(8,128)(2,1)}, bf16[512,128]{1,0:T(8,128)(2,1)S(1)}, u32[]{:S(2)}, u32[]{:S(2)}) collective-permute-start(bf16[512,128]{1,0:T(8,128)(2,1)} %get-tuple-element.11.b0), channel_id=1, source_target_pairs={{0,32},{16,48},{32,64},{48,80},{64,96},{80,112},{96,128},{112,144}... | collective-permute-start | bytes 393224 | tf_op jit(solution)/shard_map/ppermute | solution.py:339
  50.8 79.3 %all-to-all-start.3 = ((bf16[32,8,384]{2,1,0:T(8,128)(2,1)}), bf16[32,8,384]{2,1,0:T(8,128)(2,1)S(1)}, u32[]{:S(2)}, u32[]{:S(2)}) async-start(bf16[32,8,384]{2,1,0:T(8,128)(2,1)} %fusion.2), calls=%async_computation.3 | async-start | bytes 393216 | tf_op jit(solution)/shard_map/all_to_all | solution.py:287
  68.6 6.5 %collective-permute-start = (bf16[256,128]{1,0:T(8,128)(2,1)}, bf16[256,128]{1,0:T(8,128)(2,1)S(1)}, u32[]{:S(2)}, u32[]{:S(2)}) collective-permute-start(bf16[256,128]{1,0:T(8,128)(2,1)} %get-tuple-element.10), channel_id=1, source_target_pairs={{0,16},{16,0},{32,48},{48,32},{64,80},{80,64},{96,112},{112,96},{1... | collective-permute-start | bytes 196616 | tf_op jit(solution)/shard_map/ppermute | solution.py:340
  70.8 23.0 %copy-start.5 = (bf16[512,128]{1,0:T(8,128)(2,1)}, bf16[512,128]{1,0:T(8,128)(2,1)S(1)}, u32[]{:S(2)}) copy-start(bf16[512,128]{1,0:T(8,128)(2,1)S(1)} %collective-permute-done.1.b1) | copy-start | bytes 393220
  70.8 9.8 %collective-permute-start.2 = (bf16[512,128]{1,0:T(8,128)(2,1)S(1)}, bf16[512,128]{1,0:T(8,128)(2,1)S(1)}, u32[]{:S(2)}, u32[]{:S(2)}) collective-permute-start(bf16[512,128]{1,0:T(8,128)(2,1)S(1)} %collective-permute-done.1.b1), channel_id=1, source_target_pairs={{0,32},{16,48},{32,64},{48,80},{64,96},{80,112},{96,128},{112,144}... | collective-permute-start | bytes 393224 | tf_op jit(solution)/shard_map/ppermute | solution.py:339
  75.1 31.3 %copy-start.8 = (bf16[512,128]{1,0:T(8,128)(2,1)}, bf16[512,128]{1,0:T(8,128)(2,1)S(1)}, u32[]{:S(2)}) copy-start(bf16[512,128]{1,0:T(8,128)(2,1)S(1)} %constant_dynamic-update-slice_fusion.query) | copy-start | bytes 393220
  75.1 18.6 %collective-permute-start.5 = (bf16[512,128]{1,0:T(8,128)(2,1)S(1)}, bf16[512,128]{1,0:T(8,128)(2,1)S(1)}, u32[]{:S(2)}, u32[]{:S(2)}) collective-permute-start(bf16[512,128]{1,0:T(8,128)(2,1)S(1)} %constant_dynamic-update-slice_fusion.query), channel_id=1, source_target_pairs={{160,0},{176,16},{192,32},{208,48},{224,64},{240,80},{256,96},{272... | collective-permute-start | bytes 393224 | tf_op jit(solution)/shard_map/ppermute | solution.py:342
  80.6 13.2 %copy-start.6 = (bf16[512,128]{1,0:T(8,128)(2,1)}, bf16[512,128]{1,0:T(8,128)(2,1)S(1)}, u32[]{:S(2)}) copy-start(bf16[512,128]{1,0:T(8,128)(2,1)S(1)} %collective-permute-done.2.b2) | copy-start | bytes 393220
  80.6 13.2 %collective-permute-start.3 = (bf16[512,128]{1,0:T(8,128)(2,1)S(1)}, bf16[512,128]{1,0:T(8,128)(2,1)S(1)}, u32[]{:S(2)}, u32[]{:S(2)}) collective-permute-start(bf16[512,128]{1,0:T(8,128)(2,1)S(1)} %collective-permute-done.2.b2), channel_id=1, source_target_pairs={{0,32},{16,48},{32,64},{48,80},{64,96},{80,112},{96,128},{112,144}... | collective-permute-start | bytes 393224 | tf_op jit(solution)/shard_map/ppermute | solution.py:339
  93.7 0.7 copy-start.11
  94.4 0.7 copy-start.7
  98.0 12.3 %collective-permute-start.6 = (bf16[144,512]{1,0:T(8,128)(2,1)}, bf16[144,512]{1,0:T(8,128)(2,1)S(1)}, u32[]{:S(2)}, u32[]{:S(2)}) collective-permute-start(bf16[144,512]{1,0:T(8,128)(2,1)} %attend_far.1), channel_id=1, source_target_pairs={{0,160},{16,176},{32,192},{48,208},{64,224},{80,240},{96,256},{112... | collective-permute-start | bytes 442376 | tf_op jit(solution)/shard_map/ppermute | solution.py:351
  101.1 5.3 %collective-permute-start.4 = (bf16[512,128]{1,0:T(8,128)(2,1)}, bf16[512,128]{1,0:T(8,128)(2,1)S(1)}, u32[]{:S(2)}, u32[]{:S(2)}) collective-permute-start(bf16[512,128]{1,0:T(8,128)(2,1)} %copy-done.7), channel_id=1, source_target_pairs={{0,32},{16,48},{32,64},{48,80},{64,96},{80,112},{96,128},{112,144}... | collective-permute-start | bytes 393224 | tf_op jit(solution)/shard_map/ppermute | solution.py:339
  106.4 0.6 copy-start.12
  110.4 0.7 copy-start.9
  112.8 14.4 %collective-permute-start.7 = (f32[136,256]{1,0:T(8,128)}, f32[136,256]{1,0:T(8,128)S(1)}, u32[]{:S(2)}, u32[]{:S(2)}) collective-permute-start(f32[136,256]{1,0:T(8,128)} %get-tuple-element.13), channel_id=1, source_target_pairs={{0,16},{16,0},{32,48},{48,32},{64,80},{80,64},{96,112},{112,96},{1... | collective-permute-start | bytes 417800 | tf_op jit(solution)/shard_map/ppermute | solution.py:367
  127.2 0.7 copy-start.10
  130.0 20.7 %all-to-all-start.2 = ((bf16[16,256,128]{2,1,0:T(8,128)(2,1)}), bf16[16,256,128]{2,1,0:T(8,128)(2,1)S(1)}, u32[]{:S(2)}, u32[]{:S(2)}) async-start(bf16[16,256,128]{2,1,0:T(8,128)(2,1)} %finish.1), calls=%async_computation.2 | async-start | bytes 2097152 | tf_op jit(solution)/shard_map/all_to_all | solution.py:253
  150.8 1.0 copy-start.2
Sparse Core Ops, SparseCore 0:
  11.1 92.0 all-gather.2

commit v2 on v0

v2 whole, which is shorter than its diff:
```python
import jax
import jax.numpy as jnp
from jax import lax
from jax.experimental import pallas as pl
from jax.experimental.pallas import tpu as pltpu
from jax.sharding import PartitionSpec as P

MODEL_WIDTH = 2048
HEADS = 16
HEAD = 128
RANK = 16
PAGE = 8
REQS = 4
ROWS = 256
GROUPS = 32
REACH = 17
PAGES_HERE = ROWS // PAGE
WIDE = MODEL_WIDTH // 2
SIBLING = [(i, i ^ 1) for i in range(GROUPS)]
NEG = -1e30
FLOOR = -1e29
BIG = 1 << 30
SCORE_SCALE = 1.4426950408889634 * HEAD ** (-0.5)
F32 = jnp.float32
BF16 = jnp.bfloat16


def contract(a, b, dims, precision=None):
    return lax.dot_general(
        a, b, (((dims[0],), (dims[1],)), ((), ())), precision=precision, preferred_element_type=F32
    )


def iota(shape, axis):
    return lax.broadcasted_iota(jnp.int32, shape, axis)


def group():
    return lax.axis_index("gx")


def low_kernel(lengths, adapters, storage, tokens, down, out):
    rows = group() * ROWS + iota((1, ROWS), 1)
    member = lax.axis_index("gy")
    begin = jnp.int32(0)
    chosen = jnp.zeros((1, ROWS), F32)
    for r in range(REQS):
        end = begin + lengths[r]
        from_row = jnp.where(storage[adapters[r]] == member, begin, BIG)
        chosen = jnp.where((rows >= from_row) & (rows < end), 1.0, chosen)
        begin = end
    reduced = contract(down[...], tokens[...], (1, 1))
    low = jnp.where(chosen > 0.0, reduced, 0.0).astype(BF16)
    for j in range(HEADS):
        out[j] = low


def base_kernel(
    lengths, adapters, storage, tokens, weight, up, wide, base, maps, positions, dup, done
):
    core = lax.rem(group(), 2)
    half = pl.ds(pl.multiple_of(core * WIDE, WIDE), WIDE)
    copies = [pltpu.make_async_copy(wide.at[:, half], dup.at[j], done.at[j]) for j in range(HEADS)]
    for copy in copies:
        copy.start()
    rows = group() * ROWS + iota((ROWS, HEAD), 0)
    begin = jnp.zeros((ROWS, HEAD), jnp.int32)
    run = jnp.int32(0)
    for r in range(REQS - 1):
        run = run + lengths[r]
        begin = jnp.where(rows >= run, run, begin)
    positions[...] = (rows - begin).astype(F32)
    base[...] = jnp.dot(tokens[...], weight[...], preferred_element_type=F32)
    for r in range(REQS):
        slot = storage[adapters[r]]
        for c in range(3):
            maps[c, r * RANK : (r + 1) * RANK] = up[slot, c]
    for copy in copies:
        copy.wait()


def project_kernel(
    lengths, base, lows, maps, query_gain, key_gain, cosine, sine, query, keys_values, squares
):
    rows = group() * ROWS + iota((1, ROWS), 1)
    low = lows[0].astype(F32)
    for j in range(1, HEADS):
        low = low + lows[j].astype(F32)
    inside = []
    begin = jnp.int32(0)
    for r in range(REQS):
        end = begin + lengths[r]
        inside.append((rows >= begin) & (rows < end))
        begin = end
    ones = jnp.ones((8, HEAD), F32)
    values = []
    for c in range(3):
        part = low[c * RANK : (c + 1) * RANK]
        spread = jnp.concatenate([jnp.where(hit, part, 0.0) for hit in inside], axis=0).astype(BF16)
        cols = slice(c * HEAD, (c + 1) * HEAD)
        values.append(base[:, cols] + contract(spread, maps[c], (0, 0)))
    totals = [contract(ones, v * v, (1, 1), lax.Precision.HIGHEST) for v in values[:2]]
    both = jnp.where(iota((8, ROWS), 0) < 4, totals[0], totals[1])
    for j in range(HEADS):
        squares[j] = both

    def rotated(value, gain):
        value = value * gain[...]
        return value * cosine[...] + pltpu.roll(value, HEAD // 2, 1) * sine[...]

    query[...] = rotated(values[0], query_gain)
    keys_values[0:ROWS] = rotated(values[1], key_gain).astype(BF16)
    keys_values[ROWS : 2 * ROWS] = values[2].astype(BF16)


def column(line_values, pick):
    return line_values.T[:, pick : pick + 1]


def scale_kernel(raw, squares, slots, query, facts):
    total = squares[0]
    for j in range(1, HEADS):
        total = total + squares[j]
    factor = lax.rsqrt(total / MODEL_WIDTH + 1e-06)
    query[...] = (raw[...] * column(factor, 0) * SCORE_SCALE).astype(BF16)
    facts[...] = jnp.where(iota((8, ROWS), 0) == 0, slots[...].astype(F32), factor)


def normed_keys(blocks, factors):
    def one(i):
        return (blocks[i, 0:ROWS].astype(F32) * factors[:, i : i + 1]).astype(BF16)

    return one


def attend_kernel(lengths, query, facts, blocks, out, scores, held, done):
    me = group()
    first = jnp.clip(me - (REACH - 1), 0, GROUPS - REACH)
    copy = pltpu.make_async_copy(blocks.at[pl.ds(first, REACH)], held, done)
    copy.start()
    rows = me * ROWS + iota((1, ROWS), 1)
    begin = jnp.zeros((1, ROWS), jnp.int32)
    run = jnp.int32(0)
    for r in range(REQS - 1):
        run = run + lengths[r]
        begin = jnp.where(rows >= run, run, begin)
    place = iota((ROWS, ROWS), 0)
    factors = jnp.concatenate([facts[first + i, 4:5] for i in range(REACH)], axis=0).T
    key = normed_keys(held, factors)
    best = jnp.full((1, ROWS), FLOOR, F32)
    copy.wait()
    for i in range(REACH):
        score = contract(key(i), query[...], (1, 1))
        start = (first + i) * ROWS
        allowed = (place >= begin - start) & (place <= rows - start)
        score = jnp.where(allowed, score, NEG)
        scores[i] = score
        best = jnp.maximum(best, jnp.max(score, axis=0, keepdims=True))
    total = jnp.zeros((1, ROWS), F32)
    accum = jnp.zeros((HEAD, ROWS), F32)
    for i in range(REACH):
        weight = jnp.exp2(scores[i] - best)
        total = total + jnp.sum(weight, axis=0, keepdims=True)
        accum = accum + contract(held[i, ROWS : 2 * ROWS], weight.astype(BF16), (0, 0))
    attn = (accum / total).T.astype(BF16)
    for j in range(HEADS):
        out[j] = attn


def place_kernel(facts, blocks, cache, held, done):
    me = group()
    copy = pltpu.make_async_copy(blocks, held, done)
    copy.start()
    token = iota((1, ROWS), 1) & 7
    target = iota((ROWS, ROWS), 0)
    factors = jnp.concatenate([facts[i, 4:5] for i in range(GROUPS)], axis=0).T
    normed = normed_keys(held, factors)
    key = jnp.zeros((ROWS, HEAD), F32)
    value = jnp.zeros((ROWS, HEAD), F32)
    copy.wait()
    for i in range(GROUPS):
        slot = facts[i, 0:1].astype(jnp.int32)
        goes_to = jnp.where((slot >> 5) == me, (slot & 31) * PAGE + token, -1)
        pick = jnp.where(goes_to == target, 1.0, 0.0).astype(BF16)
        key = key + jnp.dot(pick, normed(i), preferred_element_type=F32)
        value = value + jnp.dot(pick, held[i, ROWS : 2 * ROWS], preferred_element_type=F32)
    cache[:, 0:HEAD] = key.astype(BF16)
    cache[:, HEAD : 2 * HEAD] = value.astype(BF16)


CHUNK = 512
AHEAD = 8


def output_kernel(attn, tokens, gain, mine, theirs, out, rows_attn, result, held, done):
    core = lax.rem(group(), 2)
    copies = []
    for side, weight in enumerate((mine, theirs)):
        for n in range(MODEL_WIDTH // CHUNK):
            rows = slice(n * CHUNK, (n + 1) * CHUNK)
            slot = done.at[side, n]
            copies.append(pltpu.make_async_copy(weight.at[rows], held.at[side, rows], slot))
    for copy in copies[:AHEAD]:
        copy.start()
    for h in range(HEADS):
        rows_attn[:, h * HEAD : (h + 1) * HEAD] = attn[h]
    square = jnp.zeros((ROWS, 1), F32)
    for side in range(2):
        for n in range(MODEL_WIDTH // CHUNK):
            rows = slice(n * CHUNK, (n + 1) * CHUNK)
            step = side * (MODEL_WIDTH // CHUNK) + n
            copies[step].wait()
            for copy in copies[step + AHEAD : step + AHEAD + 1]:
                copy.start()
            part = jnp.dot(rows_attn[:, rows], held[side, rows], preferred_element_type=F32)
            total = part if n == 0 else result[core ^ side] + part
            result[core ^ side] = total
        square = square + jnp.sum(total * total, axis=1, keepdims=True)
    scale = lax.rsqrt(square / MODEL_WIDTH + 1e-06)
    for s in range(2):
        cols = slice(s * WIDE, (s + 1) * WIDE)
        normed = result[s] * scale * gain[:, cols]
        out[:, cols] = (tokens[:, cols].astype(F32) + normed).astype(BF16)


def local(kernel, name, scalars, arrays, outs, scratch=(), stay=(), outside=()):
    specs = [pl.BlockSpec(memory_space=pltpu.SMEM)] * len(scalars)
    for n in range(len(arrays)):
        specs.append(pl.BlockSpec(memory_space=pltpu.HBM if n in stay else pltpu.VMEM))
    spaces = {True: pltpu.VMEM, False: pltpu.HBM}
    arrays = [pltpu.with_memory_space_constraint(a, spaces[near]) for near, a in arrays]
    scalars = [pltpu.with_memory_space_constraint(a, pltpu.HBM) for a in scalars]
    kinds = {True: pltpu.VMEM, False: jax.ShapeDtypeStruct, None: pltpu.HBM}
    shapes = [kinds[near](shape, dtype) for near, shape, dtype in outs]
    single = len(shapes) == 1
    out_specs = []
    for n in range(len(outs)):
        out_specs.append(pl.BlockSpec(memory_space=pltpu.HBM if n in outside else pltpu.VMEM))
    return pl.pallas_call(
        kernel,
        in_specs=specs,
        out_specs=out_specs[0] if single else out_specs,
        out_shape=shapes[0] if single else shapes,
        scratch_shapes=list(scratch),
        compiler_params=pltpu.CompilerParams(vmem_limit_bytes=16 << 20),
        name=name,
    )(*scalars, *arrays)


def exchange(copies, axis):
    return lax.all_to_all(copies, axis, split_axis=0, concat_axis=0, tiled=True)


def angles(positions):
    lane = jnp.arange(HEAD) % (HEAD // 2)
    freq = 500000.0 ** (-(lane.astype(F32) * 2.0) / HEAD)
    angle = positions * freq[None, :]
    sign = jnp.where(jnp.arange(HEAD) < HEAD // 2, -1.0, 1.0)
    return jnp.cos(angle), jnp.sin(angle) * sign[None, :]


def shards(
    tokens,
    lengths,
    adapter_of_request,
    adapter_storage_slot,
    page_cache_slot,
    query_key_value_weight,
    adapter_down_maps,
    adapter_up_maps,
    query_norm_gain,
    key_norm_gain,
    output_weight,
    post_norm_gain,
):
    together = lax.optimization_barrier
    gy = "gy"
    scalars = (lengths, adapter_of_request, adapter_storage_slot)
    lows = local(
        low_kernel,
        "low",
        scalars,
        ((False, tokens), (False, jnp.swapaxes(adapter_down_maps[0], 0, 1))),
        [(False, (HEADS, 3 * RANK, ROWS), BF16)],
    )
    lows = exchange(lows, gy)
    base, maps, positions, wide = local(
        base_kernel,
        "base",
        scalars,
        (
            (False, tokens),
            (False, query_key_value_weight[:, 0]),
            (False, adapter_up_maps[:, :, :, 0]),
            (False, output_weight[0]),
        ),
        [
            (True, (ROWS, 3 * HEAD), F32),
            (True, (3, REQS * RANK, HEAD), BF16),
            (True, (ROWS, HEAD), F32),
            (None, (HEADS, HEAD, WIDE), BF16),
        ],
        [pltpu.SemaphoreType.DMA((HEADS,))],
        (),
        (3,),
    )
    slots = jnp.repeat(page_cache_slot, PAGE)[None, :]
    cosine, sine = angles(positions)
    raw, block, squares = local(
        project_kernel,
        "project",
        scalars[:1],
        (
            (True, base),
            (True, lows),
            (True, maps),
            (False, query_norm_gain),
            (False, key_norm_gain),
            (True, cosine),
            (True, sine),
        ),
        [
            (False, (ROWS, HEAD), F32),
            (False, (2 * ROWS, HEAD), BF16),
            (False, (HEADS, 8, ROWS), F32),
        ],
    )
    blocks = lax.all_gather(block, "gx", axis=0, tiled=True).reshape(GROUPS, 2 * ROWS, HEAD)
    squares = exchange(squares, gy)
    query, facts = local(
        scale_kernel,
        "scale",
        (),
        ((True, raw), (True, squares), (True, slots)),
        [(True, (ROWS, HEAD), BF16), (True, (8, ROWS), F32)],
    )
    facts, wide = together((facts, wide))
    facts = lax.all_gather(facts, "gx", axis=0, tiled=True).reshape(GROUPS, 8, ROWS)
    mine = exchange(wide, gy).reshape(MODEL_WIDTH, WIDE)
    mine, facts = together((mine, facts))
    attn = local(
        attend_kernel,
        "attend",
        (lengths,),
        ((True, query), (True, facts), (False, blocks)),
        [(None, (HEADS, ROWS, HEAD), BF16)],
        [
            pltpu.VMEM((REACH, ROWS, ROWS), F32),
            pltpu.VMEM((REACH, 2 * ROWS, HEAD), BF16),
            pltpu.SemaphoreType.DMA,
        ],
        (2,),
    )
    attn = exchange(attn, gy)
    kv_cache = local(
        place_kernel,
        "place",
        (),
        ((True, facts), (False, blocks)),
        [(False, (ROWS, 2 * HEAD), BF16)],
        [pltpu.VMEM((GROUPS, 2 * ROWS, HEAD), BF16), pltpu.SemaphoreType.DMA],
        (1,),
    )
    theirs = lax.ppermute(mine, "gx", SIBLING)
    mixed = local(
        output_kernel,
        "project_out",
        (),
        (
            (True, attn),
            (True, tokens),
            (False, post_norm_gain[None, :]),
            (False, mine),
            (False, theirs),
        ),
        [(False, (ROWS, MODEL_WIDTH), BF16)],
        [
            pltpu.VMEM((ROWS, MODEL_WIDTH), BF16),
            pltpu.VMEM((2, ROWS, WIDE), F32),
            pltpu.VMEM((2, MODEL_WIDTH, WIDE), BF16),
            pltpu.SemaphoreType.DMA((2, MODEL_WIDTH // CHUNK)),
        ],
        (3, 4),
    )
    return (mixed, kv_cache.reshape(PAGES_HERE, PAGE, 1, 2 * HEAD))


def solution(mesh):
    return jax.shard_map(
        shards,
        mesh=mesh,
        in_specs=(
            P("gx", None),
            P(),
            P(),
            P(),
            P("gx"),
            P(None, "gy", None),
            P("gy", None, None),
            P(None, None, None, "gy", None),
            P("gy", None),
            P("gy", None),
            P("gy", None, None),
            P(),
        ),
        out_specs=(P("gx", None), P("gx", None, "gy", None)),
        check_vma=False,
    )
```

time: 446 us -> 151 us (0.34)
  waiting for transfers between devices: 257 us -> 39 us
  blocking collectives: 90.1 us -> 41 us
  matrix products: 46.3 us -> 0 us
  Pallas kernels: 0 us -> 26.5 us
  other arithmetic: 19.1 us -> 0.48 us
  starting transfers between devices: 12.8 us -> 28.5 us
    all_gather x2 -> x1, waiting for transfers between devices: 165 us -> 7.13 us  [shards(): lax.all_gather(block, 'gx', axis=0, tiled=True)]
    psum x2 -> x0, blocking collectives: 90.1 us -> none  [the longest x1 61.6 us: shards(): low = lax.psum(partial_low.astype(jnp.bfloat16), 'gy')]
    psum x1 -> x0, waiting for transfers between devices: 68 us -> none  [shards(): lax.psum(partial_out.astype(jnp.bfloat16), 'gy').astype(jnp.float32)]
    dot_general x36 -> x0, matrix products: 46.3 us -> none  [the longest x16 21.9 us: attend(): jnp.einsum('htk,khe->hte', weights.astype(jnp.bfloat16), values, preferre...]
    all_gather x0 -> x1, blocking collectives: none -> 41 us  [shards(): lax.all_gather(facts, 'gx', axis=0, tiled=True).reshape(GROUPS, 8, ROWS)]
    pallas_call x0 -> x7, Pallas kernels: none -> 26.5 us  [local(): pl.pallas_call(kernel, in_specs=specs, out_specs=out_specs[0] if single e...]
    ppermute x0 -> x1, starting transfers between devices: none -> 8.96 us  [shards(): theirs = lax.ppermute(mine, 'gx', SIBLING)]
    reduce_sum x37 -> x0, other arithmetic: 8.07 us -> none  [the longest x16 3.47 us: attend(): total = total * factor + jnp.sum(weights, axis=-1)]
  transfers between devices with their start and end apart: 5 -> 6, of which waited for: 5 -> 5; matrix products, arithmetic and copies ran while one was open for 2% -> 0% of each run, Pallas kernels for 0% -> 11%
where the time goes in v2:
time: 151 us; the launch traced here: 150 us
  blocking collectives  41 us (27%)
  waiting for transfers between devices  39 us (26%)
  starting transfers between devices  28.5 us (19%)
  Pallas kernels  26.5 us (18%)
  between operations  14.2 us (9%)
    all_gather x1, blocking collectives, shards(): lax.all_gather(facts, 'gx', axis=0, tiled=True).reshape(GROUPS, 8, ROWS)  41 us
    all_to_all x4, waiting for transfers between devices, exchange(): return lax.all_to_all(copies, axis, split_axis=0, concat_axis=0, tiled=True)  31.9 us
    pallas_call x7, Pallas kernels, local(): pl.pallas_call(kernel, in_specs=specs, out_specs=out_specs[0] if single e...  26.5 us
    all_to_all x4, starting transfers between devices, exchange(): return lax.all_to_all(copies, axis, split_axis=0, concat_axis=0, tiled=True)  19.5 us
    ppermute x1, starting transfers between devices, shards(): theirs = lax.ppermute(mine, 'gx', SIBLING)  8.96 us
    all_gather x1, waiting for transfers between devices, shards(): lax.all_gather(block, 'gx', axis=0, tiled=True)  7.13 us
  transfers between devices with their start and end apart: 6, of which 5 were waited for; matrix products, arithmetic and copies ran while one was open for 0% of the time, Pallas kernels for 11%

profile of v2, /device:TPU:1, one launch (start us, length us, event | category | flops | bytes accessed | tf_op | source)
XLA Modules:
  0.0 149.9 jit_solution(8702946251032544761)
XLA Ops:
  7.2 0.0 copy-start.1
  7.2 2.5 %low.1 = bf16[16,48,256]{2,1,0:T(8,128)(2,1)} custom-call(s32[4]{0:T(128)} %lengths.7, s32[4]{0:T(128)} %adapters.3, s32[16]{0:T(128)} %storage.3, bf16[256,2048]{1,0:T(8,128)(2,1)} %tokens.5, bf16[48,2048]{1,0:T(8,128)(2,1)} %bitcast.19), custom_call_target="tpu_custom_call" | custom-call | tf_op jit(solution)/shard_map/low/pallas_call | solution.py:239
  9.6 7.6 %all-to-all-start = ((bf16[16,48,256]{2,1,0:T(8,128)(2,1)}), bf16[16,48,256]{2,1,0:T(8,128)(2,1)S(1)}, u32[]{:S(2)}, u32[]{:S(2)}) async-start(bf16[16,48,256]{2,1,0:T(8,128)(2,1)} %low.1), calls=%async_computation | async-start | bytes 786432 | tf_op jit(solution)/shard_map/all_to_all | solution.py:251
  17.2 0.0 all-gather.2.cloned.1.call-start
  17.3 4.0 %base.1 = (f32[256,384]{1,0:T(8,128)S(1)}, bf16[3,64,128]{2,1,0:T(8,128)(2,1)S(1)}, f32[256,128]{1,0:T(8,128)S(1)}, bf16[16,128,1024]{2,1,0:T(8,128)(2,1)}) custom-call(s32[4]{0:T(128)} %lengths.7, s32[4]{0:T(128)} %adapters.3, s32[16]{0:T(128)} %storage.3, bf16[256,2048]{1,0:T(8,128)(2,1)} %tokens.5, bf16[2048,384]{1,0:T(8,128)(2,1)} %bitcast.17, ...), custom_call_target="tpu_custom_call" | custom-call | tf_op jit(solution)/shard_map/base/pallas_call | solution.py:239
  21.3 0.5 sine_multiply_fusion
  21.8 3.7 %all-to-all-done.lows = bf16[16,48,256]{2,1,0:T(8,128)(2,1)S(1)} async-done(((bf16[16,48,256]{2,1,0:T(8,128)(2,1)}), bf16[16,48,256]{2,1,0:T(8,128)(2,1)S(1)}, u32[]{:S(2)}, u32[]{:S(2)}) %all-to-all-start) | async-done | bytes 393248 | tf_op jit(solution)/shard_map/all_to_all | solution.py:251
  25.5 1.9 %project.1 = (f32[256,128]{1,0:T(8,128)S(1)}, bf16[512,128]{1,0:T(8,128)(2,1)}, f32[16,8,256]{2,1,0:T(8,128)}) custom-call(s32[4]{0:T(128)} %lengths.7, f32[256,384]{1,0:T(8,128)S(1)} %get-tuple-element.15.base, bf16[16,48,256]{2,1,0:T(8,128)(2,1)S(1)} %all-to-all-done.lows, bf16[3,64,128]{2,1,0:T(8,128)(2,1)S(1)} %get-tuple-element.16.maps, ...), custom_call_target="tpu_custom_call" | custom-call | tf_op jit(solution)/shard_map/project/pallas_call | solution.py:239
  27.4 0.0 all-gather.2.cloned.1.call-update
  27.4 3.5 %all-to-all-start.1 = ((f32[16,8,256]{2,1,0:T(8,128)}), f32[16,8,256]{2,1,0:T(8,128)S(1)}, u32[]{:S(2)}, u32[]{:S(2)}) async-start(f32[16,8,256]{2,1,0:T(8,128)} %get-tuple-element.19), calls=%async_computation.1 | async-start | bytes 262144 | tf_op jit(solution)/shard_map/all_to_all | solution.py:251
  30.9 0.0 copy-done.1
  31.0 0.1 broadcast_in_dim.18
  31.0 0.1 broadcast_in_dim_reshape.3.slots
  31.1 6.6 %all-to-all-done.1.squares = f32[16,8,256]{2,1,0:T(8,128)S(1)} async-done(((f32[16,8,256]{2,1,0:T(8,128)}), f32[16,8,256]{2,1,0:T(8,128)S(1)}, u32[]{:S(2)}, u32[]{:S(2)}) %all-to-all-start.1) | async-done | bytes 131104 | tf_op jit(solution)/shard_map/all_to_all | solution.py:251
  37.7 0.3 scale.1
  38.0 4.6 %all-to-all-start.2 = ((bf16[16,128,1024]{2,1,0:T(8,128)(2,1)}), bf16[16,128,1024]{2,1,0:T(8,128)(2,1)}, u32[]{:S(2)}, u32[]{:S(2)}) async-start(bf16[16,128,1024]{2,1,0:T(8,128)(2,1)} %get-tuple-element.23), calls=%async_computation.2 | async-start | bytes 8388608 | tf_op jit(solution)/shard_map/all_to_all | solution.py:251
  42.6 41.0 %all_gather.6 = f32[256,256]{1,0:T(8,128)S(1)} all-gather(f32[8,256]{1,0:T(8,128)S(1)} %get-tuple-element.24), channel_id=1, replica_groups=mesh['gx'=32,'gy'=16] {'gx'}, dimensions={0}, use_global_device_ids=true | all-gather | bytes 270336 | tf_op jit(solution)/shard_map/all_gather | solution.py:338
  83.6 8.8 %all-to-all-done.2 = bf16[16,128,1024]{2,1,0:T(8,128)(2,1)} async-done(((bf16[16,128,1024]{2,1,0:T(8,128)(2,1)}), bf16[16,128,1024]{2,1,0:T(8,128)(2,1)}, u32[]{:S(2)}, u32[]{:S(2)}) %all-to-all-start.2) | async-done | bytes 4194336 | tf_op jit(solution)/shard_map/all_to_all | solution.py:251
  92.4 9.0 %collective-permute-start = (bf16[2048,1024]{1,0:T(8,128)(2,1)}, bf16[2048,1024]{1,0:T(8,128)(2,1)}, u32[]{:S(2)}, u32[]{:S(2)}) collective-permute-start(bf16[2048,1024]{1,0:T(8,128)(2,1)} %bitcast.5.mine), channel_id=1, source_target_pairs={{0,16},{16,0},{32,48},{48,32},{64,80},{80,64},{96,112},{112,96},{1... | collective-permute-start | bytes 12582920 | tf_op jit(solution)/shard_map/ppermute | solution.py:364
  101.4 7.1 %all-gather.2.cloned.1.call-done = bf16[16384,128]{1,0:T(8,128)(2,1)} async-done(((bf16[512,128]{1,0:T(8,128)(2,1)}), bf16[16384,128]{1,0:T(8,128)(2,1)}) %all-gather.2.cloned.1.call-update) | async-done | bytes 4194320 | tf_op jit(solution)/shard_map/all_gather | solution.py:328
  108.5 6.3 %attend.1 = bf16[16,256,128]{2,1,0:T(8,128)(2,1)} custom-call(s32[4]{0:T(128)} %lengths.7, bf16[256,128]{1,0:T(8,128)(2,1)S(1)} %get-tuple-element.20.query, f32[32,8,256]{2,1,0:T(8,128)S(1)} %bitcast.13, bf16[32,512,128]{2,1,0:T(8,128)(2,1)} %bitcast.15), custom_call_target="tpu_custom_call" | custom-call | tf_op jit(solution)/shard_map/attend/pallas_call | solution.py:239
  114.8 0.0 copy-start
  114.8 3.8 %all-to-all-start.3 = ((bf16[16,256,128]{2,1,0:T(8,128)(2,1)}), bf16[16,256,128]{2,1,0:T(8,128)(2,1)S(1)}, u32[]{:S(2)}, u32[]{:S(2)}) async-start(bf16[16,256,128]{2,1,0:T(8,128)(2,1)} %attend.1), calls=%async_computation.3 | async-start | bytes 2097152 | tf_op jit(solution)/shard_map/all_to_all | solution.py:251
  118.6 5.4 %place.1 = bf16[256,256]{1,0:T(8,128)(2,1)} custom-call(f32[32,8,256]{2,1,0:T(8,128)S(1)} %bitcast.14, bf16[32,512,128]{2,1,0:T(8,128)(2,1)} %bitcast.16), custom_call_target="tpu_custom_call" | custom-call | tf_op jit(solution)/shard_map/place/pallas_call | solution.py:239
  124.0 0.0 collective-permute-done.theirs
  124.0 12.8 %all-to-all-done.3.attn = bf16[16,256,128]{2,1,0:T(8,128)(2,1)S(1)} async-done(((bf16[16,256,128]{2,1,0:T(8,128)(2,1)}), bf16[16,256,128]{2,1,0:T(8,128)(2,1)S(1)}, u32[]{:S(2)}, u32[]{:S(2)}) %all-to-all-start.3) | async-done | bytes 1048608 | tf_op jit(solution)/shard_map/all_to_all | solution.py:251
  136.8 0.0 copy-done
  136.8 6.2 %project_out.1 = bf16[256,2048]{1,0:T(8,128)(2,1)} custom-call(bf16[16,256,128]{2,1,0:T(8,128)(2,1)S(1)} %all-to-all-done.3.attn, bf16[256,2048]{1,0:T(8,128)(2,1)S(1)} %copy-done, f32[1,2048]{1,0:T(1,128)} %bitcast.22, bf16[2048,1024]{1,0:T(8,128)(2,1)} %bitcast.5.mine, bf16[2048,1024]{1,0:T(8,128)(2,1)} %collective-permute-done.theirs), custom_call_target="tpu_custom_call" | custom-call | tf_op jit(solution)/shard_map/project_out/pallas_call | solution.py:239
  (1 shorter events, 0.0 us)
Async XLA Ops:
  7.2 23.8 %copy-start.1 = (s32[32]{0:T(128)S(1)}, s32[32]{0:T(128)}, u32[]{:S(2)}) copy-start(s32[32]{0:T(128)} %param.16) | copy-start | bytes 388
  9.6 15.8 %all-to-all-start = ((bf16[16,48,256]{2,1,0:T(8,128)(2,1)}), bf16[16,48,256]{2,1,0:T(8,128)(2,1)S(1)}, u32[]{:S(2)}, u32[]{:S(2)}) async-start(bf16[16,48,256]{2,1,0:T(8,128)(2,1)} %low.1), calls=%async_computation | async-start | bytes 786432 | tf_op jit(solution)/shard_map/all_to_all | solution.py:251
  17.2 91.3 %all-gather.2.cloned.1.call-start = ((), (), s32[]{:S(2)}) async-start(), calls=%async_computation.4 | async-start | bytes 4325376 | tf_op jit(solution)/shard_map/all_gather | solution.py:328
  27.4 10.3 %all-to-all-start.1 = ((f32[16,8,256]{2,1,0:T(8,128)}), f32[16,8,256]{2,1,0:T(8,128)S(1)}, u32[]{:S(2)}, u32[]{:S(2)}) async-start(f32[16,8,256]{2,1,0:T(8,128)} %get-tuple-element.19), calls=%async_computation.1 | async-start | bytes 262144 | tf_op jit(solution)/shard_map/all_to_all | solution.py:251
  38.0 54.4 %all-to-all-start.2 = ((bf16[16,128,1024]{2,1,0:T(8,128)(2,1)}), bf16[16,128,1024]{2,1,0:T(8,128)(2,1)}, u32[]{:S(2)}, u32[]{:S(2)}) async-start(bf16[16,128,1024]{2,1,0:T(8,128)(2,1)} %get-tuple-element.23), calls=%async_computation.2 | async-start | bytes 8388608 | tf_op jit(solution)/shard_map/all_to_all | solution.py:251
  92.4 31.6 %collective-permute-start = (bf16[2048,1024]{1,0:T(8,128)(2,1)}, bf16[2048,1024]{1,0:T(8,128)(2,1)}, u32[]{:S(2)}, u32[]{:S(2)}) collective-permute-start(bf16[2048,1024]{1,0:T(8,128)(2,1)} %bitcast.5.mine), channel_id=1, source_target_pairs={{0,16},{16,0},{32,48},{48,32},{64,80},{80,64},{96,112},{112,96},{1... | collective-permute-start | bytes 12582920 | tf_op jit(solution)/shard_map/ppermute | solution.py:364
  114.8 22.0 %copy-start = (bf16[256,2048]{1,0:T(8,128)(2,1)S(1)}, bf16[256,2048]{1,0:T(8,128)(2,1)}, u32[]{:S(2)}) copy-start(bf16[256,2048]{1,0:T(8,128)(2,1)} %tokens.5) | copy-start | bytes 3145732
  114.8 22.0 %all-to-all-start.3 = ((bf16[16,256,128]{2,1,0:T(8,128)(2,1)}), bf16[16,256,128]{2,1,0:T(8,128)(2,1)S(1)}, u32[]{:S(2)}, u32[]{:S(2)}) async-start(bf16[16,256,128]{2,1,0:T(8,128)(2,1)} %attend.1), calls=%async_computation.3 | async-start | bytes 2097152 | tf_op jit(solution)/shard_map/all_to_all | solution.py:251
Sparse Core Ops, SparseCore 0:
  27.5 80.9 all-gather.1

commit v3 on v2

--- a/solution.py
+++ b/solution.py
@@ -14,6 +14,7 @@
 ROWS = 256
 GROUPS = 32
 REACH = 17
+FRONT = 5
 PAGES_HERE = ROWS // PAGE
 WIDE = MODEL_WIDTH // 2
 SIBLING = [(i, i ^ 1) for i in range(GROUPS)]
@@ -49,7 +50,7 @@
         from_row = jnp.where(storage[adapters[r]] == member, begin, BIG)
         chosen = jnp.where((rows >= from_row) & (rows < end), 1.0, chosen)
         begin = end
-    reduced = contract(down[...], tokens[...], (1, 1))
+    reduced = contract(tokens[...], down[...], (1, 1)).T
     low = jnp.where(chosen > 0.0, reduced, 0.0).astype(BF16)
     for j in range(HEADS):
         out[j] = low
@@ -79,38 +80,50 @@
         copy.wait()
 
 
-def project_kernel(
-    lengths, base, lows, maps, query_gain, key_gain, cosine, sine, query, keys_values, squares
-):
+def updates(lengths, lows, maps, parts):
     rows = group() * ROWS + iota((1, ROWS), 1)
-    low = lows[0].astype(F32)
+    first, last = min(parts) * RANK, (max(parts) + 1) * RANK
+    low = lows[0, first:last].astype(F32)
     for j in range(1, HEADS):
-        low = low + lows[j].astype(F32)
+        low = low + lows[j, first:last].astype(F32)
     inside = []
     begin = jnp.int32(0)
     for r in range(REQS):
         end = begin + lengths[r]
         inside.append((rows >= begin) & (rows < end))
         begin = end
+    out = []
+    for c in parts:
+        part = low[c * RANK - first : (c + 1) * RANK - first]
+        spread = jnp.concatenate([jnp.where(hit, part, 0.0) for hit in inside], axis=0).astype(BF16)
+        out.append(contract(spread, maps[c], (0, 0)))
+    return out
+
+
+def rotated(value, gain, cosine, sine):
+    value = value * gain[...]
+    return value * cosine[...] + pltpu.roll(value, HEAD // 2, 1) * sine[...]
+
+
+def keys_kernel(lengths, base, lows, maps, key_gain, cosine, sine, keys_values, key_raw):
+    key, value = updates(lengths, lows, maps, (1, 2))
+    key = key + base[:, HEAD : 2 * HEAD]
+    value = value + base[:, 2 * HEAD : 3 * HEAD]
+    key_raw[...] = key
+    keys_values[0:ROWS] = rotated(key, key_gain, cosine, sine).astype(BF16)
+    keys_values[ROWS : 2 * ROWS] = value.astype(BF16)
+
+
+def query_kernel(lengths, base, lows, maps, query_gain, cosine, sine, key_raw, query, squares):
+    (value,) = updates(lengths, lows, maps, (0,))
+    value = value + base[:, 0:HEAD]
     ones = jnp.ones((8, HEAD), F32)
-    values = []
-    for c in range(3):
-        part = low[c * RANK : (c + 1) * RANK]
-        spread = jnp.concatenate([jnp.where(hit, part, 0.0) for hit in inside], axis=0).astype(BF16)
-        cols = slice(c * HEAD, (c + 1) * HEAD)
-        values.append(base[:, cols] + contract(spread, maps[c], (0, 0)))
-    totals = [contract(ones, v * v, (1, 1), lax.Precision.HIGHEST) for v in values[:2]]
+    key = key_raw[...]
+    totals = [contract(ones, v * v, (1, 1), lax.Precision.HIGHEST) for v in (value, key)]
     both = jnp.where(iota((8, ROWS), 0) < 4, totals[0], totals[1])
     for j in range(HEADS):
         squares[j] = both
-
-    def rotated(value, gain):
-        value = value * gain[...]
-        return value * cosine[...] + pltpu.roll(value, HEAD // 2, 1) * sine[...]
-
-    query[...] = rotated(values[0], query_gain)
-    keys_values[0:ROWS] = rotated(values[1], key_gain).astype(BF16)
-    keys_values[ROWS : 2 * ROWS] = values[2].astype(BF16)
+    query[...] = rotated(value, query_gain, cosine, sine)
 
 
 def column(line_values, pick):
@@ -136,8 +149,11 @@
 def attend_kernel(lengths, query, facts, blocks, out, scores, held, done):
     me = group()
     first = jnp.clip(me - (REACH - 1), 0, GROUPS - REACH)
-    copy = pltpu.make_async_copy(blocks.at[pl.ds(first, REACH)], held, done)
-    copy.start()
+    copies = []
+    for n, (low, high) in enumerate(((0, FRONT), (FRONT, REACH))):
+        source = blocks.at[pl.ds(first + low, high - low)]
+        copies.append(pltpu.make_async_copy(source, held.at[low:high], done.at[n]))
+        copies[n].start()
     rows = me * ROWS + iota((1, ROWS), 1)
     begin = jnp.zeros((1, ROWS), jnp.int32)
     run = jnp.int32(0)
@@ -148,8 +164,10 @@
     factors = jnp.concatenate([facts[first + i, 4:5] for i in range(REACH)], axis=0).T
     key = normed_keys(held, factors)
     best = jnp.full((1, ROWS), FLOOR, F32)
-    copy.wait()
+    copies[0].wait()
     for i in range(REACH):
+        if i == FRONT:
+            copies[1].wait()
         score = contract(key(i), query[...], (1, 1))
         start = (first + i) * ROWS
         allowed = (place >= begin - start) & (place <= rows - start)
@@ -306,24 +324,34 @@
     )
     slots = jnp.repeat(page_cache_slot, PAGE)[None, :]
     cosine, sine = angles(positions)
-    raw, block, squares = local(
-        project_kernel,
-        "project",
+    block, key_raw = local(
+        keys_kernel,
+        "keys",
+        scalars[:1],
+        (
+            (True, base),
+            (True, lows),
+            (True, maps),
+            (False, key_norm_gain),
+            (True, cosine),
+            (True, sine),
+        ),
+        [(None, (2 * ROWS, HEAD), BF16), (True, (ROWS, HEAD), F32)],
+    )
+    raw, squares = local(
+        query_kernel,
+        "query",
         scalars[:1],
         (
             (True, base),
             (True, lows),
             (True, maps),
             (False, query_norm_gain),
-            (False, key_norm_gain),
             (True, cosine),
             (True, sine),
+            (True, key_raw),
         ),
-        [
-            (False, (ROWS, HEAD), F32),
-            (False, (2 * ROWS, HEAD), BF16),
-            (False, (HEADS, 8, ROWS), F32),
-        ],
+        [(False, (ROWS, HEAD), F32), (False, (HEADS, 8, ROWS), F32)],
     )
     blocks = lax.all_gather(block, "gx", axis=0, tiled=True).reshape(GROUPS, 2 * ROWS, HEAD)
     squares = exchange(squares, gy)
@@ -347,10 +375,11 @@
         [
             pltpu.VMEM((REACH, ROWS, ROWS), F32),
             pltpu.VMEM((REACH, 2 * ROWS, HEAD), BF16),
-            pltpu.SemaphoreType.DMA,
+            pltpu.SemaphoreType.DMA((2,)),
         ],
         (2,),
     )
+    mine, attn = together((mine, attn))
     attn = exchange(attn, gy)
     kv_cache = local(
         place_kernel,

time: 151 us -> 150 us (level)
  starting transfers between devices: 28.5 us -> 24.6 us
  waiting for transfers between devices: 39 us -> 40.9 us
    ppermute x1, starting transfers between devices: 8.96 us -> 2.3 us  [shards(): theirs = lax.ppermute(mine, 'gx', SIBLING)]
    all_gather x1, waiting for transfers between devices: 7.13 us -> 10.7 us  [shards(): lax.all_gather(block, 'gx', axis=0, tiled=True)]
    all_to_all x4, starting transfers between devices: 19.5 us -> 22.2 us  [exchange(): return lax.all_to_all(copies, axis, split_axis=0, concat_axis=0, tiled=True)]
    all_to_all x4, waiting for transfers between devices: 31.9 us -> 30.2 us  [exchange(): return lax.all_to_all(copies, axis, split_axis=0, concat_axis=0, tiled=True)]
    pallas_call x7 -> x8, Pallas kernels: 26.5 us -> 27.7 us  [local(): pl.pallas_call(kernel, in_specs=specs, out_specs=out_specs[0] if single e...]
  transfers between devices with their start and end apart: 6 -> 6, of which waited for: 5 -> 5; matrix products, arithmetic and copies ran while one was open for 0% -> 0% of each run, Pallas kernels for 11% -> 8%
where the time goes in v3:
time: 150 us; the launch traced here: 149 us
  blocking collectives  41 us (27%)
  waiting for transfers between devices  40.9 us (27%)
  Pallas kernels  27.7 us (18%)
  starting transfers between devices  24.6 us (16%)
  between operations  14.2 us (9%)
    all_gather x1, blocking collectives, shards(): lax.all_gather(facts, 'gx', axis=0, tiled=True).reshape(GROUPS, 8, ROWS)  41 us
    all_to_all x4, waiting for transfers between devices, exchange(): return lax.all_to_all(copies, axis, split_axis=0, concat_axis=0, tiled=True)  30.2 us
    pallas_call x8, Pallas kernels, local(): pl.pallas_call(kernel, in_specs=specs, out_specs=out_specs[0] if single e...  27.7 us
    all_to_all x4, starting transfers between devices, exchange(): return lax.all_to_all(copies, axis, split_axis=0, concat_axis=0, tiled=True)  22.2 us
    all_gather x1, waiting for transfers between devices, shards(): lax.all_gather(block, 'gx', axis=0, tiled=True)  10.7 us
  transfers between devices with their start and end apart: 6, of which 5 were waited for; matrix products, arithmetic and copies ran while one was open for 0% of the time, Pallas kernels for 8%

profile of v3, /device:TPU:1, one launch (start us, length us, event | category | flops | bytes accessed | tf_op | source)
XLA Modules:
  0.0 149.0 jit_solution(12276465790730773531)
XLA Ops:
  7.2 0.0 copy-start.1
  7.2 2.5 %low.1 = bf16[16,48,256]{2,1,0:T(8,128)(2,1)} custom-call(s32[4]{0:T(128)} %lengths.9, s32[4]{0:T(128)} %adapters.3, s32[16]{0:T(128)} %storage.3, bf16[256,2048]{1,0:T(8,128)(2,1)} %tokens.5, bf16[48,2048]{1,0:T(8,128)(2,1)} %bitcast.19), custom_call_target="tpu_custom_call" | custom-call | tf_op jit(solution)/shard_map/low/pallas_call | solution.py:257
  9.7 7.6 %all-to-all-start = ((bf16[16,48,256]{2,1,0:T(8,128)(2,1)}), bf16[16,48,256]{2,1,0:T(8,128)(2,1)S(1)}, u32[]{:S(2)}, u32[]{:S(2)}) async-start(bf16[16,48,256]{2,1,0:T(8,128)(2,1)} %low.1), calls=%async_computation | async-start | bytes 786432 | tf_op jit(solution)/shard_map/all_to_all | solution.py:269
  17.2 0.0 all-gather.2.cloned.1.call-start
  17.3 4.0 %base.1 = (f32[256,384]{1,0:T(8,128)S(1)}, bf16[3,64,128]{2,1,0:T(8,128)(2,1)S(1)}, f32[256,128]{1,0:T(8,128)S(1)}, bf16[16,128,1024]{2,1,0:T(8,128)(2,1)}) custom-call(s32[4]{0:T(128)} %lengths.9, s32[4]{0:T(128)} %adapters.3, s32[16]{0:T(128)} %storage.3, bf16[256,2048]{1,0:T(8,128)(2,1)} %tokens.5, bf16[2048,384]{1,0:T(8,128)(2,1)} %bitcast.17, ...), custom_call_target="tpu_custom_call" | custom-call | tf_op jit(solution)/shard_map/base/pallas_call | solution.py:257
  21.4 0.5 sine_multiply_fusion
  21.8 3.6 %all-to-all-done.lows = bf16[16,48,256]{2,1,0:T(8,128)(2,1)S(1)} async-done(((bf16[16,48,256]{2,1,0:T(8,128)(2,1)}), bf16[16,48,256]{2,1,0:T(8,128)(2,1)S(1)}, u32[]{:S(2)}, u32[]{:S(2)}) %all-to-all-start) | async-done | bytes 393248 | tf_op jit(solution)/shard_map/all_to_all | solution.py:269
  25.5 1.6 %keys.1 = (bf16[512,128]{1,0:T(8,128)(2,1)}, f32[256,128]{1,0:T(8,128)S(1)}) custom-call(s32[4]{0:T(128)} %lengths.9, f32[256,384]{1,0:T(8,128)S(1)} %get-tuple-element.18.base, bf16[16,48,256]{2,1,0:T(8,128)(2,1)S(1)} %all-to-all-done.lows, bf16[3,64,128]{2,1,0:T(8,128)(2,1)S(1)} %get-tuple-element.19.maps, f32[1,128]{1,0:T(1,128)} %key_gain.1, ...), custom_call_target="tpu_custom_call" | custom-call | tf_op jit(solution)/shard_map/keys/pallas_call | solution.py:257
  27.1 0.0 all-gather.2.cloned.1.call-update
  27.1 1.9 %query.1 = (f32[256,128]{1,0:T(8,128)S(1)}, f32[16,8,256]{2,1,0:T(8,128)}) custom-call(s32[4]{0:T(128)} %lengths.9, f32[256,384]{1,0:T(8,128)S(1)} %get-tuple-element.18.base, bf16[16,48,256]{2,1,0:T(8,128)(2,1)S(1)} %all-to-all-done.lows, bf16[3,64,128]{2,1,0:T(8,128)(2,1)S(1)} %get-tuple-element.19.maps, f32[1,128]{1,0:T(1,128)} %query_gain.1, ...), custom_call_target="tpu_custom_call" | custom-call | tf_op jit(solution)/shard_map/query/pallas_call | solution.py:257
  29.0 3.5 %all-to-all-start.1 = ((f32[16,8,256]{2,1,0:T(8,128)}), f32[16,8,256]{2,1,0:T(8,128)S(1)}, u32[]{:S(2)}, u32[]{:S(2)}) async-start(f32[16,8,256]{2,1,0:T(8,128)} %get-tuple-element.23), calls=%async_computation.1 | async-start | bytes 262144 | tf_op jit(solution)/shard_map/all_to_all | solution.py:269
  32.5 0.0 copy-done.1
  32.5 0.1 broadcast_in_dim.18
  32.6 0.1 broadcast_in_dim_reshape.3.slots
  32.7 6.6 %all-to-all-done.1.squares = f32[16,8,256]{2,1,0:T(8,128)S(1)} async-done(((f32[16,8,256]{2,1,0:T(8,128)}), f32[16,8,256]{2,1,0:T(8,128)S(1)}, u32[]{:S(2)}, u32[]{:S(2)}) %all-to-all-start.1) | async-done | bytes 131104 | tf_op jit(solution)/shard_map/all_to_all | solution.py:269
  39.3 0.3 scale.1
  39.6 4.5 %all-to-all-start.2 = ((bf16[16,128,1024]{2,1,0:T(8,128)(2,1)}), bf16[16,128,1024]{2,1,0:T(8,128)(2,1)}, u32[]{:S(2)}, u32[]{:S(2)}) async-start(bf16[16,128,1024]{2,1,0:T(8,128)(2,1)} %get-tuple-element.26), calls=%async_computation.2 | async-start | bytes 8388608 | tf_op jit(solution)/shard_map/all_to_all | solution.py:269
  44.2 41.0 %all_gather.6 = f32[256,256]{1,0:T(8,128)S(1)} all-gather(f32[8,256]{1,0:T(8,128)S(1)} %get-tuple-element.27), channel_id=1, replica_groups=mesh['gx'=32,'gy'=16] {'gx'}, dimensions={0}, use_global_device_ids=true | all-gather | bytes 270336 | tf_op jit(solution)/shard_map/all_gather | solution.py:366
  85.2 8.8 %all-to-all-done.2 = bf16[16,128,1024]{2,1,0:T(8,128)(2,1)} async-done(((bf16[16,128,1024]{2,1,0:T(8,128)(2,1)}), bf16[16,128,1024]{2,1,0:T(8,128)(2,1)}, u32[]{:S(2)}, u32[]{:S(2)}) %all-to-all-start.2) | async-done | bytes 4194336 | tf_op jit(solution)/shard_map/all_to_all | solution.py:269
  94.0 10.7 %all-gather.2.cloned.1.call-done = bf16[16384,128]{1,0:T(8,128)(2,1)} async-done(((bf16[512,128]{1,0:T(8,128)(2,1)}), bf16[16384,128]{1,0:T(8,128)(2,1)}) %all-gather.2.cloned.1.call-update) | async-done | bytes 4194320 | tf_op jit(solution)/shard_map/all_gather | solution.py:356
  104.7 5.8 %attend.1 = bf16[16,256,128]{2,1,0:T(8,128)(2,1)} custom-call(s32[4]{0:T(128)} %lengths.9, bf16[256,128]{1,0:T(8,128)(2,1)S(1)} %get-tuple-element.29.query, f32[32,8,256]{2,1,0:T(8,128)S(1)} %bitcast.13, bf16[32,512,128]{2,1,0:T(8,128)(2,1)} %bitcast.15), custom_call_target="tpu_custom_call" | custom-call | tf_op jit(solution)/shard_map/attend/pallas_call | solution.py:257
  110.5 0.0 copy-start
  110.5 2.3 %collective-permute-start = (bf16[2048,1024]{1,0:T(8,128)(2,1)}, bf16[2048,1024]{1,0:T(8,128)(2,1)}, u32[]{:S(2)}, u32[]{:S(2)}) collective-permute-start(bf16[2048,1024]{1,0:T(8,128)(2,1)} %bitcast.5.mine), channel_id=1, source_target_pairs={{0,16},{16,0},{32,48},{48,32},{64,80},{80,64},{96,112},{112,96},{1... | collective-permute-start | bytes 12582920 | tf_op jit(solution)/shard_map/ppermute | solution.py:393
  112.8 6.6 %all-to-all-start.3 = ((bf16[16,256,128]{2,1,0:T(8,128)(2,1)}), bf16[16,256,128]{2,1,0:T(8,128)(2,1)S(1)}, u32[]{:S(2)}, u32[]{:S(2)}) async-start(bf16[16,256,128]{2,1,0:T(8,128)(2,1)} %attend.1), calls=%async_computation.3 | async-start | bytes 2097152 | tf_op jit(solution)/shard_map/all_to_all | solution.py:269
  119.4 5.4 %place.1 = bf16[256,256]{1,0:T(8,128)(2,1)} custom-call(f32[32,8,256]{2,1,0:T(8,128)S(1)} %bitcast.14, bf16[32,512,128]{2,1,0:T(8,128)(2,1)} %bitcast.16), custom_call_target="tpu_custom_call" | custom-call | tf_op jit(solution)/shard_map/place/pallas_call | solution.py:257
  124.8 11.1 %all-to-all-done.3.attn = bf16[16,256,128]{2,1,0:T(8,128)(2,1)S(1)} async-done(((bf16[16,256,128]{2,1,0:T(8,128)(2,1)}), bf16[16,256,128]{2,1,0:T(8,128)(2,1)S(1)}, u32[]{:S(2)}, u32[]{:S(2)}) %all-to-all-start.3) | async-done | bytes 1048608 | tf_op jit(solution)/shard_map/all_to_all | solution.py:269
  135.9 0.0 collective-permute-done.theirs
  135.9 0.0 copy-done
  135.9 6.2 %project_out.1 = bf16[256,2048]{1,0:T(8,128)(2,1)} custom-call(bf16[16,256,128]{2,1,0:T(8,128)(2,1)S(1)} %all-to-all-done.3.attn, bf16[256,2048]{1,0:T(8,128)(2,1)S(1)} %copy-done, f32[1,2048]{1,0:T(1,128)} %bitcast.22, bf16[2048,1024]{1,0:T(8,128)(2,1)} %bitcast.5.mine, bf16[2048,1024]{1,0:T(8,128)(2,1)} %collective-permute-done.theirs), custom_call_target="tpu_custom_call" | custom-call | tf_op jit(solution)/shard_map/project_out/pallas_call | solution.py:257
  (1 shorter events, 0.0 us)
Async XLA Ops:
  7.2 25.4 %copy-start.1 = (s32[32]{0:T(128)S(1)}, s32[32]{0:T(128)}, u32[]{:S(2)}) copy-start(s32[32]{0:T(128)} %param.16) | copy-start | bytes 388
  9.7 15.8 %all-to-all-start = ((bf16[16,48,256]{2,1,0:T(8,128)(2,1)}), bf16[16,48,256]{2,1,0:T(8,128)(2,1)S(1)}, u32[]{:S(2)}, u32[]{:S(2)}) async-start(bf16[16,48,256]{2,1,0:T(8,128)(2,1)} %low.1), calls=%async_computation | async-start | bytes 786432 | tf_op jit(solution)/shard_map/all_to_all | solution.py:269
  17.2 87.4 %all-gather.2.cloned.1.call-start = ((), (), s32[]{:S(2)}) async-start(), calls=%async_computation.4 | async-start | bytes 4325376 | tf_op jit(solution)/shard_map/all_gather | solution.py:356
  29.0 10.3 %all-to-all-start.1 = ((f32[16,8,256]{2,1,0:T(8,128)}), f32[16,8,256]{2,1,0:T(8,128)S(1)}, u32[]{:S(2)}, u32[]{:S(2)}) async-start(f32[16,8,256]{2,1,0:T(8,128)} %get-tuple-element.23), calls=%async_computation.1 | async-start | bytes 262144 | tf_op jit(solution)/shard_map/all_to_all | solution.py:269
  39.6 54.4 %all-to-all-start.2 = ((bf16[16,128,1024]{2,1,0:T(8,128)(2,1)}), bf16[16,128,1024]{2,1,0:T(8,128)(2,1)}, u32[]{:S(2)}, u32[]{:S(2)}) async-start(bf16[16,128,1024]{2,1,0:T(8,128)(2,1)} %get-tuple-element.26), calls=%async_computation.2 | async-start | bytes 8388608 | tf_op jit(solution)/shard_map/all_to_all | solution.py:269
  110.5 25.4 %copy-start = (bf16[256,2048]{1,0:T(8,128)(2,1)S(1)}, bf16[256,2048]{1,0:T(8,128)(2,1)}, u32[]{:S(2)}) copy-start(bf16[256,2048]{1,0:T(8,128)(2,1)} %tokens.5) | copy-start | bytes 3145732
  110.5 25.4 %collective-permute-start = (bf16[2048,1024]{1,0:T(8,128)(2,1)}, bf16[2048,1024]{1,0:T(8,128)(2,1)}, u32[]{:S(2)}, u32[]{:S(2)}) collective-permute-start(bf16[2048,1024]{1,0:T(8,128)(2,1)} %bitcast.5.mine), channel_id=1, source_target_pairs={{0,16},{16,0},{32,48},{48,32},{64,80},{80,64},{96,112},{112,96},{1... | collective-permute-start | bytes 12582920 | tf_op jit(solution)/shard_map/ppermute | solution.py:393
  112.8 23.1 %all-to-all-start.3 = ((bf16[16,256,128]{2,1,0:T(8,128)(2,1)}), bf16[16,256,128]{2,1,0:T(8,128)(2,1)S(1)}, u32[]{:S(2)}, u32[]{:S(2)}) async-start(bf16[16,256,128]{2,1,0:T(8,128)(2,1)} %attend.1), calls=%async_computation.3 | async-start | bytes 2097152 | tf_op jit(solution)/shard_map/all_to_all | solution.py:269
Sparse Core Ops, SparseCore 0:
  27.3 77.3 all-gather.1

commit v4 on v3

--- a/solution.py
+++ b/solution.py
@@ -57,8 +57,33 @@
 
 
 def base_kernel(
-    lengths, adapters, storage, tokens, weight, up, wide, base, maps, positions, dup, done
+    lengths,
+    adapters,
+    storage,
+    tokens,
+    weight,
+    up,
+    wide,
+    query_gain,
+    key_gain,
+    base,
+    maps,
+    positions,
+    dup,
+    bounds,
+    gains,
+    done,
 ):
+    line = iota((8, ROWS), 0)
+    limits = jnp.zeros((8, ROWS), jnp.int32)
+    start = jnp.int32(0)
+    for r in range(REQS):
+        limits = jnp.where(line == r, start, limits)
+        start = start + lengths[r]
+        limits = jnp.where(line == REQS + r, start, limits)
+    bounds[...] = limits
+    gains[0:1] = query_gain[...]
+    gains[1:2] = key_gain[...]
     core = lax.rem(group(), 2)
     half = pl.ds(pl.multiple_of(core * WIDE, WIDE), WIDE)
     copies = [pltpu.make_async_copy(wide.at[:, half], dup.at[j], done.at[j]) for j in range(HEADS)]
@@ -80,18 +105,16 @@
         copy.wait()
 
 
-def updates(lengths, lows, maps, parts):
+def updates(bounds, lows, maps, parts):
     rows = group() * ROWS + iota((1, ROWS), 1)
     first, last = min(parts) * RANK, (max(parts) + 1) * RANK
     low = lows[0, first:last].astype(F32)
     for j in range(1, HEADS):
         low = low + lows[j, first:last].astype(F32)
     inside = []
-    begin = jnp.int32(0)
     for r in range(REQS):
-        end = begin + lengths[r]
+        begin, end = bounds[r : r + 1], bounds[REQS + r : REQS + r + 1]
         inside.append((rows >= begin) & (rows < end))
-        begin = end
     out = []
     for c in parts:
         part = low[c * RANK - first : (c + 1) * RANK - first]
@@ -101,21 +124,21 @@
 
 
 def rotated(value, gain, cosine, sine):
-    value = value * gain[...]
+    value = value * gain
     return value * cosine[...] + pltpu.roll(value, HEAD // 2, 1) * sine[...]
 
 
-def keys_kernel(lengths, base, lows, maps, key_gain, cosine, sine, keys_values, key_raw):
-    key, value = updates(lengths, lows, maps, (1, 2))
+def keys_kernel(bounds, base, lows, maps, gains, cosine, sine, keys_values, key_raw):
+    key, value = updates(bounds, lows, maps, (1, 2))
     key = key + base[:, HEAD : 2 * HEAD]
     value = value + base[:, 2 * HEAD : 3 * HEAD]
     key_raw[...] = key
-    keys_values[0:ROWS] = rotated(key, key_gain, cosine, sine).astype(BF16)
+    keys_values[0:ROWS] = rotated(key, gains[1:2], cosine, sine).astype(BF16)
     keys_values[ROWS : 2 * ROWS] = value.astype(BF16)
 
 
-def query_kernel(lengths, base, lows, maps, query_gain, cosine, sine, key_raw, query, squares):
-    (value,) = updates(lengths, lows, maps, (0,))
+def query_kernel(bounds, base, lows, maps, gains, cosine, sine, key_raw, query, squares):
+    (value,) = updates(bounds, lows, maps, (0,))
     value = value + base[:, 0:HEAD]
     ones = jnp.ones((8, HEAD), F32)
     key = key_raw[...]
@@ -123,7 +146,7 @@
     both = jnp.where(iota((8, ROWS), 0) < 4, totals[0], totals[1])
     for j in range(HEADS):
         squares[j] = both
-    query[...] = rotated(value, query_gain, cosine, sine)
+    query[...] = rotated(value, gains[0:1], cosine, sine)
 
 
 def column(line_values, pick):
@@ -146,7 +169,7 @@
     return one
 
 
-def attend_kernel(lengths, query, facts, blocks, out, scores, held, done):
+def attend_kernel(bounds, query, facts, blocks, out, scores, held, done):
     me = group()
     first = jnp.clip(me - (REACH - 1), 0, GROUPS - REACH)
     copies = []
@@ -156,10 +179,9 @@
         copies[n].start()
     rows = me * ROWS + iota((1, ROWS), 1)
     begin = jnp.zeros((1, ROWS), jnp.int32)
-    run = jnp.int32(0)
-    for r in range(REQS - 1):
-        run = run + lengths[r]
-        begin = jnp.where(rows >= run, run, begin)
+    for r in range(1, REQS):
+        start = bounds[r : r + 1]
+        begin = jnp.where(rows >= start, start, begin)
     place = iota((ROWS, ROWS), 0)
     factors = jnp.concatenate([facts[first + i, 4:5] for i in range(REACH)], axis=0).T
     key = normed_keys(held, factors)
@@ -302,7 +324,7 @@
         [(False, (HEADS, 3 * RANK, ROWS), BF16)],
     )
     lows = exchange(lows, gy)
-    base, maps, positions, wide = local(
+    base, maps, positions, wide, bounds, gains = local(
         base_kernel,
         "base",
         scalars,
@@ -311,12 +333,16 @@
             (False, query_key_value_weight[:, 0]),
             (False, adapter_up_maps[:, :, :, 0]),
             (False, output_weight[0]),
+            (False, query_norm_gain),
+            (False, key_norm_gain),
         ),
         [
             (True, (ROWS, 3 * HEAD), F32),
             (True, (3, REQS * RANK, HEAD), BF16),
             (True, (ROWS, HEAD), F32),
             (None, (HEADS, HEAD, WIDE), BF16),
+            (True, (8, ROWS), jnp.int32),
+            (True, (2, HEAD), F32),
         ],
         [pltpu.SemaphoreType.DMA((HEADS,))],
         (),
@@ -327,12 +353,13 @@
     block, key_raw = local(
         keys_kernel,
         "keys",
-        scalars[:1],
+        (),
         (
+            (True, bounds),
             (True, base),
             (True, lows),
             (True, maps),
-            (False, key_norm_gain),
+            (True, gains),
             (True, cosine),
             (True, sine),
         ),
@@ -341,12 +368,13 @@
     raw, squares = local(
         query_kernel,
         "query",
-        scalars[:1],
+        (),
         (
+            (True, bounds),
             (True, base),
             (True, lows),
             (True, maps),
-            (False, query_norm_gain),
+            (True, gains),
             (True, cosine),
             (True, sine),
             (True, key_raw),
@@ -369,15 +397,15 @@
     attn = local(
         attend_kernel,
         "attend",
-        (lengths,),
-        ((True, query), (True, facts), (False, blocks)),
+        (),
+        ((True, bounds), (True, query), (True, facts), (False, blocks)),
         [(None, (HEADS, ROWS, HEAD), BF16)],
         [
             pltpu.VMEM((REACH, ROWS, ROWS), F32),
             pltpu.VMEM((REACH, 2 * ROWS, HEAD), BF16),
             pltpu.SemaphoreType.DMA((2,)),
         ],
-        (2,),
+        (3,),
     )
     mine, attn = together((mine, attn))
     attn = exchange(attn, gy)
@@ -398,7 +426,7 @@
         (
             (True, attn),
             (True, tokens),
-            (False, post_norm_gain[None, :]),
+            (True, post_norm_gain[None, :]),
             (False, mine),
             (False, theirs),
         ),

time: 150 us -> 147 us (0.980)
  Pallas kernels: 27.7 us -> 25.1 us
    pallas_call x8, Pallas kernels: 27.7 us -> 25.1 us  [local(): pl.pallas_call(kernel, in_specs=specs, out_specs=out_specs[0] if single e...]
  transfers between devices with their start and end apart: 6 -> 6, of which waited for: 5 -> 5; matrix products, arithmetic and copies ran while one was open for 0% -> 0% of each run, Pallas kernels for 8% -> 7%
where the time goes in v4:
time: 147 us
  waiting for transfers between devices  42 us (29%)
  blocking collectives  40.8 us (28%)
  Pallas kernels  25.1 us (17%)
  starting transfers between devices  24.2 us (16%)
  between operations  14.2 us (10%)
    all_gather x1, blocking collectives, shards(): lax.all_gather(facts, 'gx', axis=0, tiled=True).reshape(GROUPS, 8, ROWS)  40.8 us
    all_to_all x4, waiting for transfers between devices, exchange(): return lax.all_to_all(copies, axis, split_axis=0, concat_axis=0, tiled=True)  30.3 us
    pallas_call x8, Pallas kernels, local(): pl.pallas_call(kernel, in_specs=specs, out_specs=out_specs[0] if single e...  25.1 us
    all_to_all x4, starting transfers between devices, exchange(): return lax.all_to_all(copies, axis, split_axis=0, concat_axis=0, tiled=True)  21.8 us
    all_gather x1, waiting for transfers between devices, shards(): lax.all_gather(block, 'gx', axis=0, tiled=True)  11.7 us
  transfers between devices with their start and end apart: 6, of which 5 were waited for; matrix products, arithmetic and copies ran while one was open for 0% of the time, Pallas kernels for 7%

profile of v4, /device:TPU:1, one launch (start us, length us, event | category | flops | bytes accessed | tf_op | source)
XLA Modules:
  0.0 146.9 jit_solution(17403659945400024878)
XLA Ops:
  7.2 0.0 copy-start.2
  7.2 2.5 %low.1 = bf16[16,48,256]{2,1,0:T(8,128)(2,1)} custom-call(s32[4]{0:T(128)} %lengths.3, s32[4]{0:T(128)} %adapters.3, s32[16]{0:T(128)} %storage.3, bf16[256,2048]{1,0:T(8,128)(2,1)} %tokens.5, bf16[48,2048]{1,0:T(8,128)(2,1)} %bitcast.21), custom_call_target="tpu_custom_call" | custom-call | tf_op jit(solution)/shard_map/low/pallas_call | solution.py:279
  9.7 7.6 %all-to-all-start = ((bf16[16,48,256]{2,1,0:T(8,128)(2,1)}), bf16[16,48,256]{2,1,0:T(8,128)(2,1)S(1)}, u32[]{:S(2)}, u32[]{:S(2)}) async-start(bf16[16,48,256]{2,1,0:T(8,128)(2,1)} %low.1), calls=%async_computation | async-start | bytes 786432 | tf_op jit(solution)/shard_map/all_to_all | solution.py:291
  17.2 0.0 all-gather.2.cloned.1.call-start
  17.3 4.2 %base.1 = (f32[256,384]{1,0:T(8,128)S(1)}, bf16[3,64,128]{2,1,0:T(8,128)(2,1)S(1)}, f32[256,128]{1,0:T(8,128)S(1)}, bf16[16,128,1024]{2,1,0:T(8,128)(2,1)}, s32[8,256]{1,0:T(8,128)S(1)}, /*index=5*/f32[2,128]{1,0:T(2,128)S(1)}) custom-call(s32[4]{0:T(128)} %lengths.3, s32[4]{0:T(128)} %adapters.3, s32[16]{0:T(128)} %storage.3, bf16[256,2048]{1,0:T(8,128)(2,1)} %tokens.5, ...), custom_call_target="tpu_custom_call" | custom-call | tf_op jit(solution)/shard_map/base/pallas_call | solution.py:279
  21.5 0.5 sine_multiply_fusion
  22.0 3.5 %all-to-all-done.lows = bf16[16,48,256]{2,1,0:T(8,128)(2,1)S(1)} async-done(((bf16[16,48,256]{2,1,0:T(8,128)(2,1)}), bf16[16,48,256]{2,1,0:T(8,128)(2,1)S(1)}, u32[]{:S(2)}, u32[]{:S(2)}) %all-to-all-start) | async-done | bytes 393248 | tf_op jit(solution)/shard_map/all_to_all | solution.py:291
  25.5 1.0 keys.1
  26.4 0.0 all-gather.2.cloned.1.call-update
  26.5 1.2 query.1
  27.7 3.5 %all-to-all-start.1 = ((f32[16,8,256]{2,1,0:T(8,128)}), f32[16,8,256]{2,1,0:T(8,128)S(1)}, u32[]{:S(2)}, u32[]{:S(2)}) async-start(f32[16,8,256]{2,1,0:T(8,128)} %get-tuple-element.27), calls=%async_computation.1 | async-start | bytes 262144 | tf_op jit(solution)/shard_map/all_to_all | solution.py:291
  31.2 0.0 copy-done.2
  31.2 0.1 broadcast_in_dim.18
  31.3 0.1 broadcast_in_dim_reshape.3.slots
  31.4 6.6 %all-to-all-done.1.squares = f32[16,8,256]{2,1,0:T(8,128)S(1)} async-done(((f32[16,8,256]{2,1,0:T(8,128)}), f32[16,8,256]{2,1,0:T(8,128)S(1)}, u32[]{:S(2)}, u32[]{:S(2)}) %all-to-all-start.1) | async-done | bytes 131104 | tf_op jit(solution)/shard_map/all_to_all | solution.py:291
  38.0 0.3 scale.1
  38.3 4.6 %all-to-all-start.2 = ((bf16[16,128,1024]{2,1,0:T(8,128)(2,1)}), bf16[16,128,1024]{2,1,0:T(8,128)(2,1)}, u32[]{:S(2)}, u32[]{:S(2)}) async-start(bf16[16,128,1024]{2,1,0:T(8,128)(2,1)} %get-tuple-element.30), calls=%async_computation.2 | async-start | bytes 8388608 | tf_op jit(solution)/shard_map/all_to_all | solution.py:291
  42.8 40.8 %all_gather.6 = f32[256,256]{1,0:T(8,128)S(1)} all-gather(f32[8,256]{1,0:T(8,128)S(1)} %get-tuple-element.31), channel_id=1, replica_groups=mesh['gx'=32,'gy'=16] {'gx'}, dimensions={0}, use_global_device_ids=true | all-gather | bytes 270336 | tf_op jit(solution)/shard_map/all_gather | solution.py:394
  83.6 9.0 %all-to-all-done.2 = bf16[16,128,1024]{2,1,0:T(8,128)(2,1)} async-done(((bf16[16,128,1024]{2,1,0:T(8,128)(2,1)}), bf16[16,128,1024]{2,1,0:T(8,128)(2,1)}, u32[]{:S(2)}, u32[]{:S(2)}) %all-to-all-start.2) | async-done | bytes 4194336 | tf_op jit(solution)/shard_map/all_to_all | solution.py:291
  92.7 11.7 %all-gather.2.cloned.1.call-done = bf16[16384,128]{1,0:T(8,128)(2,1)} async-done(((bf16[512,128]{1,0:T(8,128)(2,1)}), bf16[16384,128]{1,0:T(8,128)(2,1)}) %all-gather.2.cloned.1.call-update) | async-done | bytes 4194320 | tf_op jit(solution)/shard_map/all_gather | solution.py:384
  104.3 5.1 %attend.1 = bf16[16,256,128]{2,1,0:T(8,128)(2,1)} custom-call(s32[8,256]{1,0:T(8,128)S(1)} %get-tuple-element.20.bounds, bf16[256,128]{1,0:T(8,128)(2,1)S(1)} %get-tuple-element.33.query, f32[32,8,256]{2,1,0:T(8,128)S(1)} %bitcast.13, bf16[32,512,128]{2,1,0:T(8,128)(2,1)} %bitcast.16), custom_call_target="tpu_custom_call" | custom-call | tf_op jit(solution)/shard_map/attend/pallas_call | solution.py:279
  109.5 0.0 copy-start
  109.5 0.0 copy-start.1
  109.5 2.3 %collective-permute-start = (bf16[2048,1024]{1,0:T(8,128)(2,1)}, bf16[2048,1024]{1,0:T(8,128)(2,1)}, u32[]{:S(2)}, u32[]{:S(2)}) collective-permute-start(bf16[2048,1024]{1,0:T(8,128)(2,1)} %bitcast.5.mine), channel_id=1, source_target_pairs={{0,16},{16,0},{32,48},{48,32},{64,80},{80,64},{96,112},{112,96},{1... | collective-permute-start | bytes 12582920 | tf_op jit(solution)/shard_map/ppermute | solution.py:421
  111.8 6.2 %all-to-all-start.3 = ((bf16[16,256,128]{2,1,0:T(8,128)(2,1)}), bf16[16,256,128]{2,1,0:T(8,128)(2,1)S(1)}, u32[]{:S(2)}, u32[]{:S(2)}) async-start(bf16[16,256,128]{2,1,0:T(8,128)(2,1)} %attend.1), calls=%async_computation.3 | async-start | bytes 2097152 | tf_op jit(solution)/shard_map/all_to_all | solution.py:291
  118.0 5.4 %place.1 = bf16[256,256]{1,0:T(8,128)(2,1)} custom-call(f32[32,8,256]{2,1,0:T(8,128)S(1)} %bitcast.14, bf16[32,512,128]{2,1,0:T(8,128)(2,1)} %bitcast.17), custom_call_target="tpu_custom_call" | custom-call | tf_op jit(solution)/shard_map/place/pallas_call | solution.py:279
  123.4 11.1 %all-to-all-done.3.attn = bf16[16,256,128]{2,1,0:T(8,128)(2,1)S(1)} async-done(((bf16[16,256,128]{2,1,0:T(8,128)(2,1)}), bf16[16,256,128]{2,1,0:T(8,128)(2,1)S(1)}, u32[]{:S(2)}, u32[]{:S(2)}) %all-to-all-start.3) | async-done | bytes 1048608 | tf_op jit(solution)/shard_map/all_to_all | solution.py:291
  134.5 0.0 collective-permute-done.theirs
  134.5 0.0 copy-done
  134.5 0.0 copy-done.1
  134.5 5.5 %project_out.1 = bf16[256,2048]{1,0:T(8,128)(2,1)} custom-call(bf16[16,256,128]{2,1,0:T(8,128)(2,1)S(1)} %all-to-all-done.3.attn, bf16[256,2048]{1,0:T(8,128)(2,1)S(1)} %copy-done, f32[1,2048]{1,0:T(1,128)S(1)} %bitcast.15, bf16[2048,1024]{1,0:T(8,128)(2,1)} %bitcast.5.mine, bf16[2048,1024]{1,0:T(8,128)(2,1)} %collective-permute-done.theirs), custom_call_target="tpu_custom_call" | custom-call | tf_op jit(solution)/shard_map/project_out/pallas_call | solution.py:279
  (1 shorter events, 0.0 us)
Async XLA Ops:
  7.2 24.0 %copy-start.2 = (s32[32]{0:T(128)S(1)}, s32[32]{0:T(128)}, u32[]{:S(2)}) copy-start(s32[32]{0:T(128)} %param.16) | copy-start | bytes 388
  9.7 15.8 %all-to-all-start = ((bf16[16,48,256]{2,1,0:T(8,128)(2,1)}), bf16[16,48,256]{2,1,0:T(8,128)(2,1)S(1)}, u32[]{:S(2)}, u32[]{:S(2)}) async-start(bf16[16,48,256]{2,1,0:T(8,128)(2,1)} %low.1), calls=%async_computation | async-start | bytes 786432 | tf_op jit(solution)/shard_map/all_to_all | solution.py:291
  17.2 87.1 %all-gather.2.cloned.1.call-start = ((), (), s32[]{:S(2)}) async-start(), calls=%async_computation.4 | async-start | bytes 4325376 | tf_op jit(solution)/shard_map/all_gather | solution.py:384
  27.7 10.3 %all-to-all-start.1 = ((f32[16,8,256]{2,1,0:T(8,128)}), f32[16,8,256]{2,1,0:T(8,128)S(1)}, u32[]{:S(2)}, u32[]{:S(2)}) async-start(f32[16,8,256]{2,1,0:T(8,128)} %get-tuple-element.27), calls=%async_computation.1 | async-start | bytes 262144 | tf_op jit(solution)/shard_map/all_to_all | solution.py:291
  38.3 54.4 %all-to-all-start.2 = ((bf16[16,128,1024]{2,1,0:T(8,128)(2,1)}), bf16[16,128,1024]{2,1,0:T(8,128)(2,1)}, u32[]{:S(2)}, u32[]{:S(2)}) async-start(bf16[16,128,1024]{2,1,0:T(8,128)(2,1)} %get-tuple-element.30), calls=%async_computation.2 | async-start | bytes 8388608 | tf_op jit(solution)/shard_map/all_to_all | solution.py:291
  109.5 25.0 %copy-start = (bf16[256,2048]{1,0:T(8,128)(2,1)S(1)}, bf16[256,2048]{1,0:T(8,128)(2,1)}, u32[]{:S(2)}) copy-start(bf16[256,2048]{1,0:T(8,128)(2,1)} %tokens.5) | copy-start | bytes 3145732
  109.5 25.0 %copy-start.1 = (f32[2048]{0:T(1024)S(1)}, f32[2048]{0:T(1024)}, u32[]{:S(2)}) copy-start(f32[2048]{0:T(1024)} %param.23) | copy-start | bytes 24580
  109.5 25.0 %collective-permute-start = (bf16[2048,1024]{1,0:T(8,128)(2,1)}, bf16[2048,1024]{1,0:T(8,128)(2,1)}, u32[]{:S(2)}, u32[]{:S(2)}) collective-permute-start(bf16[2048,1024]{1,0:T(8,128)(2,1)} %bitcast.5.mine), channel_id=1, source_target_pairs={{0,16},{16,0},{32,48},{48,32},{64,80},{80,64},{96,112},{112,96},{1... | collective-permute-start | bytes 12582920 | tf_op jit(solution)/shard_map/ppermute | solution.py:421
  111.8 22.7 %all-to-all-start.3 = ((bf16[16,256,128]{2,1,0:T(8,128)(2,1)}), bf16[16,256,128]{2,1,0:T(8,128)(2,1)S(1)}, u32[]{:S(2)}, u32[]{:S(2)}) async-start(bf16[16,256,128]{2,1,0:T(8,128)(2,1)} %attend.1), calls=%async_computation.3 | async-start | bytes 2097152 | tf_op jit(solution)/shard_map/all_to_all | solution.py:291
Sparse Core Ops, SparseCore 0:
  26.6 77.7 all-gather.1
